TPU v7x, 512 devices: a whole 4x8x8 slice. The times are simulated.
512 devices in a mesh: mem: 16 (over y, core), lat: 8 (over x, z_hi), lon: 4 (over z_lo).
Axes of the slice: x: 4, y: 8, z: 8 (z_hi: 2, z_lo: 4; z = z_hi * 4 + z_lo), core: 2. Of those that a mesh axis runs over, the one named last changes fastest.
Arguments:
- members: bfloat16 [32, 8, 256, 512], P('mem', None, 'lat', 'lon'), may hold values from -6 to 6
- increment: float32 [8, 256, 512], P(None, 'lat', 'lon'), may hold values from -6 to 6
Outputs:
- covariance_product: float32 [8, 256, 512], P(None, 'lat', 'lon')
All inputs are finite; a program needn't handle non-finite values.
Results may differ from a plain program's by a relative error of at most 0.0003.
Values sent between devices are 32-bit elements; how exact they have to be, the bound alone decides.
No kernel may reach another device: no remote copies, remote signals or barrier semaphores. Data moves between devices by JAX's collectives and lax.ppermute only.
A program may use at most 64 MiB of HBM per device.

v0:
```python
import jax
import jax.numpy as jnp
from jax import lax
from jax.sharding import PartitionSpec as P

ITERS = 4


factors = (1, 2, 4)
stiffnesses = (1.0, 2.0, 4.0)
weights = (0.5, 0.3, 0.2)


def with_halo(block, sides, width, periodic):
    for axis, dim in sides:
        count = lax.axis_size(axis)
        forward = [(i, i + 1) for i in range(count - 1)]
        if periodic:
            forward.append((count - 1, 0))
        backward = [(target, source) for source, target in forward]
        low = lax.ppermute(
            lax.slice_in_dim(block, block.shape[dim] - width, None, axis=dim), axis, forward
        )
        high = lax.ppermute(lax.slice_in_dim(block, 0, width, axis=dim), axis, backward)
        block = jnp.concatenate([low, block, high], axis=dim)
    return block


def coarsen(values_now, factor):
    if factor == 1:
        return values_now
    dims_now = values_now.shape
    blocks = values_now.reshape(
        dims_now[:-2] + (dims_now[-2] // factor, factor, dims_now[-1] // factor, factor)
    )
    return jnp.mean(blocks, axis=(-3, -1))


def refine(values_now, factor):
    if factor == 1:
        return values_now
    return jnp.repeat(jnp.repeat(values_now, factor, axis=-2), factor, axis=-1)


def diffuse_single(source, stiffness):
    smoothed = source
    for sweeps in range(ITERS):
        with_rows = with_halo(smoothed, (("lat", 2),), 1, False)
        with_cols = with_halo(smoothed, (("lon", 3),), 1, True)
        beside_all = with_rows[:, :, :-2, :] + with_rows[:, :, 2:, :]
        beside_all = beside_all + with_cols[:, :, :, :-2] + with_cols[:, :, :, 2:]
        smoothed = (source + stiffness * beside_all) / (1.0 + 4.0 * stiffness)
    return smoothed


def body(members, increment):
    member_field = members.astype(jnp.float32)
    product = member_field * increment[None]
    running = jnp.zeros(member_field.shape, jnp.float32)
    for factor, stiffness, weight in zip(factors, stiffnesses, weights):
        source = coarsen(product, factor)
        coarse = diffuse_single(source, stiffness)
        running = running + weight * member_field * refine(coarse, factor)
    partial_value = jnp.sum(running, axis=0)
    member_count = members.shape[0] * lax.axis_size("mem")
    summed = lax.psum(partial_value, "mem")
    return summed / (member_count - 1)


def solution(mesh):
    return jax.shard_map(
        body,
        mesh=mesh,
        in_specs=(P("mem", None, "lat", "lon"), P(None, "lat", "lon")),
        out_specs=P(None, "lat", "lon"),
        check_vma=False,
    )
```

profile of v0, /device:TPU:7, one launch (start us, length us, event | category | flops | bytes accessed | tf_op | source)
XLA Modules:
  0.0 434.0 jit_solution(4924736812012016826)
XLA Ops:
  9.0 4.3 copy.364
  13.3 5.6 %reduce_sum.27 = f32[2,8,16,64]{1,3,2,0:T(8,128)S(1)} reduce(f32[2,8,16,2,64,2]{1,5,4,3,2,0:T(2,128)} %bitcast.6, f32[]{:T(128)} %constant.30.clone.1), dimensions={3,5}, to_apply=%region_0.0 | reduce | flops 49152 | bytes 327684 | tf_op jit(solution)/shard_map/reduce_sum | solution.py:36
  20.1 7.6 %collective-permute-start.19 = (f32[2,8,16,1]{3,2,1,0:T(8,128)}, f32[2,8,16,1]{3,2,1,0:T(8,128)}, u32[]{:S(2)}, u32[]{:S(2)}) collective-permute-start(f32[2,8,16,1]{3,2,1,0:T(8,128)} %get-tuple-element.52), channel_id=1, source_target_pairs={{1,0},{2,1},{3,2},{0,3},{5,4},{6,5},{7,6},{4,7},{9,8},{10,9},{11,1... | collective-permute-start | bytes 3080 | tf_op jit(solution)/shard_map/ppermute | solution.py:24
  27.7 3.6 reduce_sum.28
  33.3 3.4 collective-permute-start.34
  36.6 8.2 %collective-permute-start.33 = (f32[2,8,1,32]{1,3,2,0:T(8,128)S(1)}, f32[2,8,1,32]{1,3,2,0:T(8,128)S(1)}, u32[]{:S(2)}, u32[]{:S(2)}) collective-permute-start(f32[2,8,1,32]{1,3,2,0:T(8,128)S(1)} %get-tuple-element.34), channel_id=1, source_target_pairs={{4,0},{8,4},{12,8},{16,12},{20,16},{24,20},{28,24},{5,1},{9,5},{13... | collective-permute-start | bytes 6152 | tf_op jit(solution)/shard_map/ppermute | solution.py:24
  49.6 4.7 %collective-permute-done.32 = f32[2,8,1,32]{1,3,2,0:T(8,128)S(1)} collective-permute-done((f32[2,8,1,32]{1,3,2,0:T(8,128)S(1)}, f32[2,8,1,32]{1,3,2,0:T(8,128)S(1)}, u32[]{:S(2)}, u32[]{:S(2)}) %collective-permute-start.32) | collective-permute-done | bytes 2080 | tf_op jit(solution)/shard_map/ppermute | solution.py:21
  55.8 4.1 collective-permute-start.39
  61.8 3.4 collective-permute-start.37
  65.2 6.4 %collective-permute-start.36 = (f32[2,8,1,32]{1,3,2,0:T(8,128)}, f32[2,8,1,32]{1,3,2,0:T(8,128)}, u32[]{:S(2)}, u32[]{:S(2)}) collective-permute-start(f32[2,8,1,32]{1,3,2,0:T(8,128)} %get-tuple-element.29), channel_id=1, source_target_pairs={{0,4},{4,8},{8,12},{12,16},{16,20},{20,24},{24,28},{1,5},{5,9},{9,... | collective-permute-start | bytes 6152 | tf_op jit(solution)/shard_map/ppermute | solution.py:21
  72.2 2.2 copy.350
  76.6 3.7 collective-permute-start.17
  80.4 5.5 %collective-permute-start.16 = (f32[2,8,1,64]{3,2,1,0:T(1,128)}, f32[2,8,1,64]{3,2,1,0:T(1,128)S(1)}, u32[]{:S(2)}, u32[]{:S(2)}) collective-permute-start(f32[2,8,1,64]{3,2,1,0:T(1,128)} %get-tuple-element.49), channel_id=1, source_target_pairs={{0,4},{4,8},{8,12},{12,16},{16,20},{20,24},{24,28},{1,5},{5,9},{9,... | collective-permute-start | bytes 12296 | tf_op jit(solution)/shard_map/ppermute | solution.py:21
  85.8 5.2 %collective-permute-start.3 = (f32[2,8,32,1]{2,1,3,0:T(8,128)}, f32[2,8,32,1]{2,1,3,0:T(8,128)S(1)}, u32[]{:S(2)}, u32[]{:S(2)}) collective-permute-start(f32[2,8,32,1]{2,1,3,0:T(8,128)} %get-tuple-element.20), channel_id=1, source_target_pairs={{1,0},{2,1},{3,2},{0,3},{5,4},{6,5},{7,6},{4,7},{9,8},{10,9},{11,1... | collective-permute-start | bytes 6152 | tf_op jit(solution)/shard_map/ppermute | solution.py:24
  94.2 3.4 collective-permute-start.43
  99.5 4.6 %collective-permute-start.41 = (f32[2,8,1,32]{1,3,2,0:T(8,128)S(1)}, f32[2,8,1,32]{1,3,2,0:T(8,128)S(1)}, u32[]{:S(2)}, u32[]{:S(2)}) collective-permute-start(f32[2,8,1,32]{1,3,2,0:T(8,128)S(1)} %get-tuple-element.26), channel_id=1, source_target_pairs={{4,0},{8,4},{12,8},{16,12},{20,16},{24,20},{28,24},{5,1},{9,5},{13... | collective-permute-start | bytes 6152 | tf_op jit(solution)/shard_map/ppermute | solution.py:24
  104.1 4.6 %collective-permute-start.40 = (f32[2,8,1,32]{1,3,2,0:T(8,128)S(1)}, f32[2,8,1,32]{1,3,2,0:T(8,128)S(1)}, u32[]{:S(2)}, u32[]{:S(2)}) collective-permute-start(f32[2,8,1,32]{1,3,2,0:T(8,128)S(1)} %get-tuple-element.25), channel_id=1, source_target_pairs={{0,4},{4,8},{8,12},{12,16},{16,20},{20,24},{24,28},{1,5},{5,9},{9,... | collective-permute-start | bytes 6152 | tf_op jit(solution)/shard_map/ppermute | solution.py:21
  108.7 5.2 %collective-permute-start.23 = (f32[2,8,16,1]{3,2,1,0:T(8,128)S(1)}, f32[2,8,16,1]{3,2,1,0:T(8,128)S(1)}, u32[]{:S(2)}, u32[]{:S(2)}) collective-permute-start(f32[2,8,16,1]{3,2,1,0:T(8,128)S(1)} %get-tuple-element.48), channel_id=1, source_target_pairs={{1,0},{2,1},{3,2},{0,3},{5,4},{6,5},{7,6},{4,7},{9,8},{10,9},{11,1... | collective-permute-start | bytes 3080 | tf_op jit(solution)/shard_map/ppermute | solution.py:24
  115.9 5.5 %collective-permute-start.21 = (f32[2,8,1,64]{3,2,1,0:T(1,128)S(1)}, f32[2,8,1,64]{3,2,1,0:T(1,128)S(1)}, u32[]{:S(2)}, u32[]{:S(2)}) collective-permute-start(f32[2,8,1,64]{3,2,1,0:T(1,128)S(1)} %get-tuple-element.46), channel_id=1, source_target_pairs={{4,0},{8,4},{12,8},{16,12},{20,16},{24,20},{28,24},{5,1},{9,5},{13... | collective-permute-start | bytes 12296 | tf_op jit(solution)/shard_map/ppermute | solution.py:24
  121.4 3.7 collective-permute-start.20
  128.4 6.4 %collective-permute-start.1 = (f32[2,8,1,128]{3,1,2,0:T(8,128)}, f32[2,8,1,128]{3,1,2,0:T(8,128)S(1)}, u32[]{:S(2)}, u32[]{:S(2)}) collective-permute-start(f32[2,8,1,128]{3,1,2,0:T(8,128)} %copy.350), channel_id=1, source_target_pairs={{4,0},{8,4},{12,8},{16,12},{20,16},{24,20},{28,24},{5,1},{9,5},{13... | collective-permute-start | bytes 24584 | tf_op jit(solution)/shard_map/ppermute | solution.py:24
  134.9 2.8 collective-permute-start
  137.7 5.2 %collective-permute-start.47 = (f32[2,8,8,1]{1,3,2,0:T(1,128)}, f32[2,8,8,1]{1,3,2,0:T(1,128)}, u32[]{:S(2)}, u32[]{:S(2)}) collective-permute-start(f32[2,8,8,1]{1,3,2,0:T(1,128)} %get-tuple-element.24), channel_id=1, source_target_pairs={{1,0},{2,1},{3,2},{0,3},{5,4},{6,5},{7,6},{4,7},{9,8},{10,9},{11,1... | collective-permute-start | bytes 1544 | tf_op jit(solution)/shard_map/ppermute | solution.py:24
  147.1 7.3 %collective-permute-start.45 = (f32[2,8,1,32]{1,3,2,0:T(8,128)}, f32[2,8,1,32]{1,3,2,0:T(8,128)}, u32[]{:S(2)}, u32[]{:S(2)}) collective-permute-start(f32[2,8,1,32]{1,3,2,0:T(8,128)} %get-tuple-element.22), channel_id=1, source_target_pairs={{4,0},{8,4},{12,8},{16,12},{20,16},{24,20},{28,24},{5,1},{9,5},{13... | collective-permute-start | bytes 6152 | tf_op jit(solution)/shard_map/ppermute | solution.py:24
  155.8 2.4 collective-permute-start.44
  158.9 5.3 %collective-permute-start.27 = (f32[2,8,16,1]{3,2,1,0:T(8,128)}, f32[2,8,16,1]{3,2,1,0:T(8,128)}, u32[]{:S(2)}, u32[]{:S(2)}) collective-permute-start(f32[2,8,16,1]{3,2,1,0:T(8,128)} %get-tuple-element.44), channel_id=1, source_target_pairs={{1,0},{2,1},{3,2},{0,3},{5,4},{6,5},{7,6},{4,7},{9,8},{10,9},{11,1... | collective-permute-start | bytes 3080 | tf_op jit(solution)/shard_map/ppermute | solution.py:24
  164.2 2.5 fusion.23
  171.5 7.6 %collective-permute-start.25 = (f32[2,8,1,64]{3,2,1,0:T(1,128)}, f32[2,8,1,64]{3,2,1,0:T(1,128)S(1)}, u32[]{:S(2)}, u32[]{:S(2)}) collective-permute-start(f32[2,8,1,64]{3,2,1,0:T(1,128)} %get-tuple-element.42), channel_id=1, source_target_pairs={{4,0},{8,4},{12,8},{16,12},{20,16},{24,20},{28,24},{5,1},{9,5},{13... | collective-permute-start | bytes 12296 | tf_op jit(solution)/shard_map/ppermute | solution.py:24
  186.7 5.1 %collective-permute-start.7 = (f32[2,8,32,1]{2,1,3,0:T(8,128)}, f32[2,8,32,1]{2,1,3,0:T(8,128)S(1)}, u32[]{:S(2)}, u32[]{:S(2)}) collective-permute-start(f32[2,8,32,1]{2,1,3,0:T(8,128)} %get-tuple-element.16), channel_id=1, source_target_pairs={{1,0},{2,1},{3,2},{0,3},{5,4},{6,5},{7,6},{4,7},{9,8},{10,9},{11,1... | collective-permute-start | bytes 6152 | tf_op jit(solution)/shard_map/ppermute | solution.py:24
  191.8 2.1 copy.354
  196.9 8.2 %collective-permute-start.5 = (f32[2,8,1,128]{3,1,2,0:T(8,128)}, f32[2,8,1,128]{3,1,2,0:T(8,128)S(1)}, u32[]{:S(2)}, u32[]{:S(2)}) collective-permute-start(f32[2,8,1,128]{3,1,2,0:T(8,128)} %copy.354), channel_id=1, source_target_pairs={{4,0},{8,4},{12,8},{16,12},{20,16},{24,20},{28,24},{5,1},{9,5},{13... | collective-permute-start | bytes 24584 | tf_op jit(solution)/shard_map/ppermute | solution.py:24
  210.5 4.0 collective-permute-done.4
  215.8 2.4 fusion.18
  220.3 5.2 %collective-permute-start.11 = (f32[2,8,32,1]{2,1,3,0:T(8,128)}, f32[2,8,32,1]{2,1,3,0:T(8,128)S(1)}, u32[]{:S(2)}, u32[]{:S(2)}) collective-permute-start(f32[2,8,32,1]{2,1,3,0:T(8,128)} %get-tuple-element.12), channel_id=1, source_target_pairs={{1,0},{2,1},{3,2},{0,3},{5,4},{6,5},{7,6},{4,7},{9,8},{10,9},{11,1... | collective-permute-start | bytes 6152 | tf_op jit(solution)/shard_map/ppermute | solution.py:24
  227.4 2.2 copy.358
  229.5 4.1 collective-permute-start.9
  234.6 5.0 %collective-permute-start.8 = (f32[2,8,1,128]{3,1,2,0:T(8,128)}, f32[2,8,1,128]{3,1,2,0:T(8,128)S(1)}, u32[]{:S(2)}, u32[]{:S(2)}) collective-permute-start(f32[2,8,1,128]{3,1,2,0:T(8,128)} %copy.356), channel_id=1, source_target_pairs={{0,4},{4,8},{8,12},{12,16},{16,20},{20,24},{24,28},{1,5},{5,9},{9,... | collective-permute-start | bytes 24584 | tf_op jit(solution)/shard_map/ppermute | solution.py:21
  240.3 5.2 %collective-permute-start.31 = (f32[2,8,16,1]{3,2,1,0:T(8,128)}, f32[2,8,16,1]{3,2,1,0:T(8,128)}, u32[]{:S(2)}, u32[]{:S(2)}) collective-permute-start(f32[2,8,16,1]{3,2,1,0:T(8,128)} %get-tuple-element.40), channel_id=1, source_target_pairs={{1,0},{2,1},{3,2},{0,3},{5,4},{6,5},{7,6},{4,7},{9,8},{10,9},{11,1... | collective-permute-start | bytes 3080 | tf_op jit(solution)/shard_map/ppermute | solution.py:24
  248.8 5.0 %collective-permute-start.29 = (f32[2,8,1,64]{3,2,1,0:T(1,128)}, f32[2,8,1,64]{3,2,1,0:T(1,128)S(1)}, u32[]{:S(2)}, u32[]{:S(2)}) collective-permute-start(f32[2,8,1,64]{3,2,1,0:T(1,128)} %get-tuple-element.38), channel_id=1, source_target_pairs={{4,0},{8,4},{12,8},{16,12},{20,16},{24,20},{28,24},{5,1},{9,5},{13... | collective-permute-start | bytes 12296 | tf_op jit(solution)/shard_map/ppermute | solution.py:24
  255.2 4.1 collective-permute-start.28
  259.4 2.4 fusion.13
  263.8 5.1 %collective-permute-start.15 = (f32[2,8,32,1]{2,1,3,0:T(8,128)}, f32[2,8,32,1]{2,1,3,0:T(8,128)S(1)}, u32[]{:S(2)}, u32[]{:S(2)}) collective-permute-start(f32[2,8,32,1]{2,1,3,0:T(8,128)} %get-tuple-element.8), channel_id=1, source_target_pairs={{1,0},{2,1},{3,2},{0,3},{5,4},{6,5},{7,6},{4,7},{9,8},{10,9},{11,1... | collective-permute-start | bytes 6152 | tf_op jit(solution)/shard_map/ppermute | solution.py:24
  268.9 2.1 copy.362
  273.9 5.9 %collective-permute-start.13 = (f32[2,8,1,128]{3,1,2,0:T(8,128)}, f32[2,8,1,128]{3,1,2,0:T(8,128)}, u32[]{:S(2)}, u32[]{:S(2)}) collective-permute-start(f32[2,8,1,128]{3,1,2,0:T(8,128)} %copy.362), channel_id=1, source_target_pairs={{4,0},{8,4},{12,8},{16,12},{20,16},{24,20},{28,24},{5,1},{9,5},{13... | collective-permute-start | bytes 24584 | tf_op jit(solution)/shard_map/ppermute | solution.py:24
  279.9 3.8 collective-permute-start.12
  287.1 2.3 collective-permute-done.12
  292.7 3.2 fusion.3
  297.8 127.8 %all-reduce.2.cloned.1.call-done = f32[8,32,128]{2,1,0:T(8,128)} async-done(((f32[8,32,128]{2,1,0:T(8,128)}), f32[8,32,128]{2,1,0:T(8,128)}) %all-reduce.2.cloned.1.call-update) | async-done | bytes 131088 | tf_op jit(solution)/shard_map/psum | solution.py:66
  (138 shorter events, 80.0 us)
Async XLA Ops:
  6.5 419.0 %all-reduce.2.cloned.1.call-start = ((), (), s32[]{:S(2)}) async-start(), calls=%async_computation | async-start | bytes 262144 | tf_op jit(solution)/shard_map/psum | solution.py:66
  20.1 72.4 %collective-permute-start.19 = (f32[2,8,16,1]{3,2,1,0:T(8,128)}, f32[2,8,16,1]{3,2,1,0:T(8,128)}, u32[]{:S(2)}, u32[]{:S(2)}) collective-permute-start(f32[2,8,16,1]{3,2,1,0:T(8,128)} %get-tuple-element.52), channel_id=1, source_target_pairs={{1,0},{2,1},{3,2},{0,3},{5,4},{6,5},{7,6},{4,7},{9,8},{10,9},{11,1... | collective-permute-start | bytes 3080 | tf_op jit(solution)/shard_map/ppermute | solution.py:24
  31.3 18.3 %collective-permute-start.35 = (f32[2,8,8,1]{1,3,2,0:T(1,128)S(1)}, f32[2,8,8,1]{1,3,2,0:T(1,128)S(1)}, u32[]{:S(2)}, u32[]{:S(2)}) collective-permute-start(f32[2,8,8,1]{1,3,2,0:T(1,128)S(1)} %get-tuple-element.36), channel_id=1, source_target_pairs={{1,0},{2,1},{3,2},{0,3},{5,4},{6,5},{7,6},{4,7},{9,8},{10,9},{11,1... | collective-permute-start | bytes 1544 | tf_op jit(solution)/shard_map/ppermute | solution.py:24
  33.3 16.4 %collective-permute-start.34 = (f32[2,8,8,1]{1,3,2,0:T(1,128)S(1)}, f32[2,8,8,1]{1,3,2,0:T(1,128)S(1)}, u32[]{:S(2)}, u32[]{:S(2)}) collective-permute-start(f32[2,8,8,1]{1,3,2,0:T(1,128)S(1)} %get-tuple-element.35), channel_id=1, source_target_pairs={{0,1},{1,2},{2,3},{3,0},{4,5},{5,6},{6,7},{7,4},{8,9},{9,10},{10,1... | collective-permute-start | bytes 1544 | tf_op jit(solution)/shard_map/ppermute | solution.py:21
  36.6 13.0 %collective-permute-start.33 = (f32[2,8,1,32]{1,3,2,0:T(8,128)S(1)}, f32[2,8,1,32]{1,3,2,0:T(8,128)S(1)}, u32[]{:S(2)}, u32[]{:S(2)}) collective-permute-start(f32[2,8,1,32]{1,3,2,0:T(8,128)S(1)} %get-tuple-element.34), channel_id=1, source_target_pairs={{4,0},{8,4},{12,8},{16,12},{20,16},{24,20},{28,24},{5,1},{9,5},{13... | collective-permute-start | bytes 6152 | tf_op jit(solution)/shard_map/ppermute | solution.py:24
  44.9 9.5 %collective-permute-start.32 = (f32[2,8,1,32]{1,3,2,0:T(8,128)S(1)}, f32[2,8,1,32]{1,3,2,0:T(8,128)S(1)}, u32[]{:S(2)}, u32[]{:S(2)}) collective-permute-start(f32[2,8,1,32]{1,3,2,0:T(8,128)S(1)} %get-tuple-element.33), channel_id=1, source_target_pairs={{0,4},{4,8},{8,12},{12,16},{16,20},{20,24},{24,28},{1,5},{5,9},{9,... | collective-permute-start | bytes 6152 | tf_op jit(solution)/shard_map/ppermute | solution.py:21
  55.8 18.9 %collective-permute-start.39 = (f32[2,8,8,1]{1,3,2,0:T(1,128)}, f32[2,8,8,1]{1,3,2,0:T(1,128)S(1)}, u32[]{:S(2)}, u32[]{:S(2)}) collective-permute-start(f32[2,8,8,1]{1,3,2,0:T(1,128)} %get-tuple-element.32), channel_id=1, source_target_pairs={{1,0},{2,1},{3,2},{0,3},{5,4},{6,5},{7,6},{4,7},{9,8},{10,9},{11,1... | collective-permute-start | bytes 1544 | tf_op jit(solution)/shard_map/ppermute | solution.py:24
  59.8 16.8 %collective-permute-start.38 = (f32[2,8,8,1]{1,3,2,0:T(1,128)}, f32[2,8,8,1]{1,3,2,0:T(1,128)}, u32[]{:S(2)}, u32[]{:S(2)}) collective-permute-start(f32[2,8,8,1]{1,3,2,0:T(1,128)} %get-tuple-element.31), channel_id=1, source_target_pairs={{0,1},{1,2},{2,3},{3,0},{4,5},{5,6},{6,7},{7,4},{8,9},{9,10},{10,1... | collective-permute-start | bytes 1544 | tf_op jit(solution)/shard_map/ppermute | solution.py:21
  61.8 18.6 %collective-permute-start.37 = (f32[2,8,1,32]{1,3,2,0:T(8,128)}, f32[2,8,1,32]{1,3,2,0:T(8,128)}, u32[]{:S(2)}, u32[]{:S(2)}) collective-permute-start(f32[2,8,1,32]{1,3,2,0:T(8,128)} %get-tuple-element.30), channel_id=1, source_target_pairs={{4,0},{8,4},{12,8},{16,12},{20,16},{24,20},{28,24},{5,1},{9,5},{13... | collective-permute-start | bytes 6152 | tf_op jit(solution)/shard_map/ppermute | solution.py:24
  65.2 20.6 %collective-permute-start.36 = (f32[2,8,1,32]{1,3,2,0:T(8,128)}, f32[2,8,1,32]{1,3,2,0:T(8,128)}, u32[]{:S(2)}, u32[]{:S(2)}) collective-permute-start(f32[2,8,1,32]{1,3,2,0:T(8,128)} %get-tuple-element.29), channel_id=1, source_target_pairs={{0,4},{4,8},{8,12},{12,16},{16,20},{20,24},{24,28},{1,5},{5,9},{9,... | collective-permute-start | bytes 6152 | tf_op jit(solution)/shard_map/ppermute | solution.py:21
  74.7 17.8 %collective-permute-start.18 = (f32[2,8,16,1]{3,2,1,0:T(8,128)}, f32[2,8,16,1]{3,2,1,0:T(8,128)S(1)}, u32[]{:S(2)}, u32[]{:S(2)}) collective-permute-start(f32[2,8,16,1]{3,2,1,0:T(8,128)} %get-tuple-element.51), channel_id=1, source_target_pairs={{0,1},{1,2},{2,3},{3,0},{4,5},{5,6},{6,7},{7,4},{8,9},{9,10},{10,1... | collective-permute-start | bytes 3080 | tf_op jit(solution)/shard_map/ppermute | solution.py:21
  76.6 15.9 %collective-permute-start.17 = (f32[2,8,1,64]{3,2,1,0:T(1,128)}, f32[2,8,1,64]{3,2,1,0:T(1,128)S(1)}, u32[]{:S(2)}, u32[]{:S(2)}) collective-permute-start(f32[2,8,1,64]{3,2,1,0:T(1,128)} %get-tuple-element.50), channel_id=1, source_target_pairs={{4,0},{8,4},{12,8},{16,12},{20,16},{24,20},{28,24},{5,1},{9,5},{13... | collective-permute-start | bytes 12296 | tf_op jit(solution)/shard_map/ppermute | solution.py:24
  80.4 12.2 %collective-permute-start.16 = (f32[2,8,1,64]{3,2,1,0:T(1,128)}, f32[2,8,1,64]{3,2,1,0:T(1,128)S(1)}, u32[]{:S(2)}, u32[]{:S(2)}) collective-permute-start(f32[2,8,1,64]{3,2,1,0:T(1,128)} %get-tuple-element.49), channel_id=1, source_target_pairs={{0,4},{4,8},{8,12},{12,16},{16,20},{20,24},{24,28},{1,5},{5,9},{9,... | collective-permute-start | bytes 12296 | tf_op jit(solution)/shard_map/ppermute | solution.py:21
  85.8 70.0 %collective-permute-start.3 = (f32[2,8,32,1]{2,1,3,0:T(8,128)}, f32[2,8,32,1]{2,1,3,0:T(8,128)S(1)}, u32[]{:S(2)}, u32[]{:S(2)}) collective-permute-start(f32[2,8,32,1]{2,1,3,0:T(8,128)} %get-tuple-element.20), channel_id=1, source_target_pairs={{1,0},{2,1},{3,2},{0,3},{5,4},{6,5},{7,6},{4,7},{9,8},{10,9},{11,1... | collective-permute-start | bytes 6152 | tf_op jit(solution)/shard_map/ppermute | solution.py:24
  94.2 14.5 %collective-permute-start.43 = (f32[2,8,8,1]{1,3,2,0:T(1,128)S(1)}, f32[2,8,8,1]{1,3,2,0:T(1,128)S(1)}, u32[]{:S(2)}, u32[]{:S(2)}) collective-permute-start(f32[2,8,8,1]{1,3,2,0:T(1,128)S(1)} %get-tuple-element.28), channel_id=1, source_target_pairs={{1,0},{2,1},{3,2},{0,3},{5,4},{6,5},{7,6},{4,7},{9,8},{10,9},{11,1... | collective-permute-start | bytes 1544 | tf_op jit(solution)/shard_map/ppermute | solution.py:24
  97.6 16.3 %collective-permute-start.42 = (f32[2,8,8,1]{1,3,2,0:T(1,128)S(1)}, f32[2,8,8,1]{1,3,2,0:T(1,128)S(1)}, u32[]{:S(2)}, u32[]{:S(2)}) collective-permute-start(f32[2,8,8,1]{1,3,2,0:T(1,128)S(1)} %get-tuple-element.27), channel_id=1, source_target_pairs={{0,1},{1,2},{2,3},{3,0},{4,5},{5,6},{6,7},{7,4},{8,9},{9,10},{10,1... | collective-permute-start | bytes 1544 | tf_op jit(solution)/shard_map/ppermute | solution.py:21
  99.5 16.3 %collective-permute-start.41 = (f32[2,8,1,32]{1,3,2,0:T(8,128)S(1)}, f32[2,8,1,32]{1,3,2,0:T(8,128)S(1)}, u32[]{:S(2)}, u32[]{:S(2)}) collective-permute-start(f32[2,8,1,32]{1,3,2,0:T(8,128)S(1)} %get-tuple-element.26), channel_id=1, source_target_pairs={{4,0},{8,4},{12,8},{16,12},{20,16},{24,20},{28,24},{5,1},{9,5},{13... | collective-permute-start | bytes 6152 | tf_op jit(solution)/shard_map/ppermute | solution.py:24
  104.1 17.3 %collective-permute-start.40 = (f32[2,8,1,32]{1,3,2,0:T(8,128)S(1)}, f32[2,8,1,32]{1,3,2,0:T(8,128)S(1)}, u32[]{:S(2)}, u32[]{:S(2)}) collective-permute-start(f32[2,8,1,32]{1,3,2,0:T(8,128)S(1)} %get-tuple-element.25), channel_id=1, source_target_pairs={{0,4},{4,8},{8,12},{12,16},{16,20},{20,24},{24,28},{1,5},{5,9},{9,... | collective-permute-start | bytes 6152 | tf_op jit(solution)/shard_map/ppermute | solution.py:21
  108.7 17.8 %collective-permute-start.23 = (f32[2,8,16,1]{3,2,1,0:T(8,128)S(1)}, f32[2,8,16,1]{3,2,1,0:T(8,128)S(1)}, u32[]{:S(2)}, u32[]{:S(2)}) collective-permute-start(f32[2,8,16,1]{3,2,1,0:T(8,128)S(1)} %get-tuple-element.48), channel_id=1, source_target_pairs={{1,0},{2,1},{3,2},{0,3},{5,4},{6,5},{7,6},{4,7},{9,8},{10,9},{11,1... | collective-permute-start | bytes 3080 | tf_op jit(solution)/shard_map/ppermute | solution.py:24
  113.9 14.5 %collective-permute-start.22 = (f32[2,8,16,1]{3,2,1,0:T(8,128)S(1)}, f32[2,8,16,1]{3,2,1,0:T(8,128)S(1)}, u32[]{:S(2)}, u32[]{:S(2)}) collective-permute-start(f32[2,8,16,1]{3,2,1,0:T(8,128)S(1)} %get-tuple-element.47), channel_id=1, source_target_pairs={{0,1},{1,2},{2,3},{3,0},{4,5},{5,6},{6,7},{7,4},{8,9},{9,10},{10,1... | collective-permute-start | bytes 3080 | tf_op jit(solution)/shard_map/ppermute | solution.py:21
  115.9 19.0 %collective-permute-start.21 = (f32[2,8,1,64]{3,2,1,0:T(1,128)S(1)}, f32[2,8,1,64]{3,2,1,0:T(1,128)S(1)}, u32[]{:S(2)}, u32[]{:S(2)}) collective-permute-start(f32[2,8,1,64]{3,2,1,0:T(1,128)S(1)} %get-tuple-element.46), channel_id=1, source_target_pairs={{4,0},{8,4},{12,8},{16,12},{20,16},{24,20},{28,24},{5,1},{9,5},{13... | collective-permute-start | bytes 12296 | tf_op jit(solution)/shard_map/ppermute | solution.py:24
  121.4 16.2 %collective-permute-start.20 = (f32[2,8,1,64]{3,2,1,0:T(1,128)S(1)}, f32[2,8,1,64]{3,2,1,0:T(1,128)S(1)}, u32[]{:S(2)}, u32[]{:S(2)}) collective-permute-start(f32[2,8,1,64]{3,2,1,0:T(1,128)S(1)} %get-tuple-element.45), channel_id=1, source_target_pairs={{0,4},{4,8},{8,12},{12,16},{16,20},{20,24},{24,28},{1,5},{5,9},{9,... | collective-permute-start | bytes 12296 | tf_op jit(solution)/shard_map/ppermute | solution.py:21
  126.5 31.7 %collective-permute-start.2 = (f32[2,8,32,1]{2,1,3,0:T(8,128)}, f32[2,8,32,1]{2,1,3,0:T(8,128)S(1)}, u32[]{:S(2)}, u32[]{:S(2)}) collective-permute-start(f32[2,8,32,1]{2,1,3,0:T(8,128)} %get-tuple-element.19), channel_id=1, source_target_pairs={{0,1},{1,2},{2,3},{3,0},{4,5},{5,6},{6,7},{7,4},{8,9},{9,10},{10,1... | collective-permute-start | bytes 6152 | tf_op jit(solution)/shard_map/ppermute | solution.py:21
  128.4 15.4 %collective-permute-start.1 = (f32[2,8,1,128]{3,1,2,0:T(8,128)}, f32[2,8,1,128]{3,1,2,0:T(8,128)S(1)}, u32[]{:S(2)}, u32[]{:S(2)}) collective-permute-start(f32[2,8,1,128]{3,1,2,0:T(8,128)} %copy.350), channel_id=1, source_target_pairs={{4,0},{8,4},{12,8},{16,12},{20,16},{24,20},{28,24},{5,1},{9,5},{13... | collective-permute-start | bytes 24584 | tf_op jit(solution)/shard_map/ppermute | solution.py:24
  134.9 12.2 %collective-permute-start = (f32[2,8,1,128]{3,1,2,0:T(8,128)S(1)}, f32[2,8,1,128]{3,1,2,0:T(8,128)S(1)}, u32[]{:S(2)}, u32[]{:S(2)}) collective-permute-start(f32[2,8,1,128]{3,1,2,0:T(8,128)S(1)} %copy.348), channel_id=1, source_target_pairs={{0,4},{4,8},{8,12},{12,16},{16,20},{20,24},{24,28},{1,5},{5,9},{9,... | collective-permute-start | bytes 24584 | tf_op jit(solution)/shard_map/ppermute | solution.py:21
  137.7 31.9 %collective-permute-start.47 = (f32[2,8,8,1]{1,3,2,0:T(1,128)}, f32[2,8,8,1]{1,3,2,0:T(1,128)}, u32[]{:S(2)}, u32[]{:S(2)}) collective-permute-start(f32[2,8,8,1]{1,3,2,0:T(1,128)} %get-tuple-element.24), channel_id=1, source_target_pairs={{1,0},{2,1},{3,2},{0,3},{5,4},{6,5},{7,6},{4,7},{9,8},{10,9},{11,1... | collective-permute-start | bytes 1544 | tf_op jit(solution)/shard_map/ppermute | solution.py:24
  143.8 27.7 %collective-permute-start.46 = (f32[2,8,8,1]{1,3,2,0:T(1,128)}, f32[2,8,8,1]{1,3,2,0:T(1,128)}, u32[]{:S(2)}, u32[]{:S(2)}) collective-permute-start(f32[2,8,8,1]{1,3,2,0:T(1,128)} %get-tuple-element.23), channel_id=1, source_target_pairs={{0,1},{1,2},{2,3},{3,0},{4,5},{5,6},{6,7},{7,4},{8,9},{9,10},{10,1... | collective-permute-start | bytes 1544 | tf_op jit(solution)/shard_map/ppermute | solution.py:21
  147.1 32.0 %collective-permute-start.45 = (f32[2,8,1,32]{1,3,2,0:T(8,128)}, f32[2,8,1,32]{1,3,2,0:T(8,128)}, u32[]{:S(2)}, u32[]{:S(2)}) collective-permute-start(f32[2,8,1,32]{1,3,2,0:T(8,128)} %get-tuple-element.22), channel_id=1, source_target_pairs={{4,0},{8,4},{12,8},{16,12},{20,16},{24,20},{28,24},{5,1},{9,5},{13... | collective-permute-start | bytes 6152 | tf_op jit(solution)/shard_map/ppermute | solution.py:24
  155.8 25.2 %collective-permute-start.44 = (f32[2,8,1,32]{1,3,2,0:T(8,128)}, f32[2,8,1,32]{1,3,2,0:T(8,128)S(1)}, u32[]{:S(2)}, u32[]{:S(2)}) collective-permute-start(f32[2,8,1,32]{1,3,2,0:T(8,128)} %get-tuple-element.21), channel_id=1, source_target_pairs={{0,4},{4,8},{8,12},{12,16},{16,20},{20,24},{24,28},{1,5},{5,9},{9,... | collective-permute-start | bytes 6152 | tf_op jit(solution)/shard_map/ppermute | solution.py:21
  158.9 36.1 %collective-permute-start.27 = (f32[2,8,16,1]{3,2,1,0:T(8,128)}, f32[2,8,16,1]{3,2,1,0:T(8,128)}, u32[]{:S(2)}, u32[]{:S(2)}) collective-permute-start(f32[2,8,16,1]{3,2,1,0:T(8,128)} %get-tuple-element.44), channel_id=1, source_target_pairs={{1,0},{2,1},{3,2},{0,3},{5,4},{6,5},{7,6},{4,7},{9,8},{10,9},{11,1... | collective-permute-start | bytes 3080 | tf_op jit(solution)/shard_map/ppermute | solution.py:24
  169.5 27.3 %collective-permute-start.26 = (f32[2,8,16,1]{3,2,1,0:T(8,128)}, f32[2,8,16,1]{3,2,1,0:T(8,128)}, u32[]{:S(2)}, u32[]{:S(2)}) collective-permute-start(f32[2,8,16,1]{3,2,1,0:T(8,128)} %get-tuple-element.43), channel_id=1, source_target_pairs={{0,1},{1,2},{2,3},{3,0},{4,5},{5,6},{6,7},{7,4},{8,9},{9,10},{10,1... | collective-permute-start | bytes 3080 | tf_op jit(solution)/shard_map/ppermute | solution.py:21
  171.5 33.6 %collective-permute-start.25 = (f32[2,8,1,64]{3,2,1,0:T(1,128)}, f32[2,8,1,64]{3,2,1,0:T(1,128)S(1)}, u32[]{:S(2)}, u32[]{:S(2)}) collective-permute-start(f32[2,8,1,64]{3,2,1,0:T(1,128)} %get-tuple-element.42), channel_id=1, source_target_pairs={{4,0},{8,4},{12,8},{16,12},{20,16},{24,20},{28,24},{5,1},{9,5},{13... | collective-permute-start | bytes 12296 | tf_op jit(solution)/shard_map/ppermute | solution.py:24
  179.1 27.9 %collective-permute-start.24 = (f32[2,8,1,64]{3,2,1,0:T(1,128)}, f32[2,8,1,64]{3,2,1,0:T(1,128)}, u32[]{:S(2)}, u32[]{:S(2)}) collective-permute-start(f32[2,8,1,64]{3,2,1,0:T(1,128)} %get-tuple-element.41), channel_id=1, source_target_pairs={{0,4},{4,8},{8,12},{12,16},{16,20},{20,24},{24,28},{1,5},{5,9},{9,... | collective-permute-start | bytes 12296 | tf_op jit(solution)/shard_map/ppermute | solution.py:21
  186.7 29.2 %collective-permute-start.7 = (f32[2,8,32,1]{2,1,3,0:T(8,128)}, f32[2,8,32,1]{2,1,3,0:T(8,128)S(1)}, u32[]{:S(2)}, u32[]{:S(2)}) collective-permute-start(f32[2,8,32,1]{2,1,3,0:T(8,128)} %get-tuple-element.16), channel_id=1, source_target_pairs={{1,0},{2,1},{3,2},{0,3},{5,4},{6,5},{7,6},{4,7},{9,8},{10,9},{11,1... | collective-permute-start | bytes 6152 | tf_op jit(solution)/shard_map/ppermute | solution.py:24
  195.0 20.9 %collective-permute-start.6 = (f32[2,8,32,1]{2,1,3,0:T(8,128)}, f32[2,8,32,1]{2,1,3,0:T(8,128)}, u32[]{:S(2)}, u32[]{:S(2)}) collective-permute-start(f32[2,8,32,1]{2,1,3,0:T(8,128)} %get-tuple-element.15), channel_id=1, source_target_pairs={{0,1},{1,2},{2,3},{3,0},{4,5},{5,6},{6,7},{7,4},{8,9},{9,10},{10,1... | collective-permute-start | bytes 6152 | tf_op jit(solution)/shard_map/ppermute | solution.py:21
  196.9 12.2 %collective-permute-start.5 = (f32[2,8,1,128]{3,1,2,0:T(8,128)}, f32[2,8,1,128]{3,1,2,0:T(8,128)S(1)}, u32[]{:S(2)}, u32[]{:S(2)}) collective-permute-start(f32[2,8,1,128]{3,1,2,0:T(8,128)} %copy.354), channel_id=1, source_target_pairs={{4,0},{8,4},{12,8},{16,12},{20,16},{24,20},{28,24},{5,1},{9,5},{13... | collective-permute-start | bytes 24584 | tf_op jit(solution)/shard_map/ppermute | solution.py:24
  220.3 34.9 %collective-permute-start.11 = (f32[2,8,32,1]{2,1,3,0:T(8,128)}, f32[2,8,32,1]{2,1,3,0:T(8,128)S(1)}, u32[]{:S(2)}, u32[]{:S(2)}) collective-permute-start(f32[2,8,32,1]{2,1,3,0:T(8,128)} %get-tuple-element.12), channel_id=1, source_target_pairs={{1,0},{2,1},{3,2},{0,3},{5,4},{6,5},{7,6},{4,7},{9,8},{10,9},{11,1... | collective-permute-start | bytes 6152 | tf_op jit(solution)/shard_map/ppermute | solution.py:24
  225.5 33.9 %collective-permute-start.10 = (f32[2,8,32,1]{2,1,3,0:T(8,128)}, f32[2,8,32,1]{2,1,3,0:T(8,128)}, u32[]{:S(2)}, u32[]{:S(2)}) collective-permute-start(f32[2,8,32,1]{2,1,3,0:T(8,128)} %get-tuple-element.11), channel_id=1, source_target_pairs={{0,1},{1,2},{2,3},{3,0},{4,5},{5,6},{6,7},{7,4},{8,9},{9,10},{10,1... | collective-permute-start | bytes 6152 | tf_op jit(solution)/shard_map/ppermute | solution.py:21
  229.5 15.9 %collective-permute-start.9 = (f32[2,8,1,128]{3,1,2,0:T(8,128)}, f32[2,8,1,128]{3,1,2,0:T(8,128)S(1)}, u32[]{:S(2)}, u32[]{:S(2)}) collective-permute-start(f32[2,8,1,128]{3,1,2,0:T(8,128)} %copy.358), channel_id=1, source_target_pairs={{4,0},{8,4},{12,8},{16,12},{20,16},{24,20},{28,24},{5,1},{9,5},{13... | collective-permute-start | bytes 24584 | tf_op jit(solution)/shard_map/ppermute | solution.py:24
  234.6 14.2 %collective-permute-start.8 = (f32[2,8,1,128]{3,1,2,0:T(8,128)}, f32[2,8,1,128]{3,1,2,0:T(8,128)S(1)}, u32[]{:S(2)}, u32[]{:S(2)}) collective-permute-start(f32[2,8,1,128]{3,1,2,0:T(8,128)} %copy.356), channel_id=1, source_target_pairs={{0,4},{4,8},{8,12},{12,16},{16,20},{20,24},{24,28},{1,5},{5,9},{9,... | collective-permute-start | bytes 24584 | tf_op jit(solution)/shard_map/ppermute | solution.py:21
  240.3 31.7 %collective-permute-start.31 = (f32[2,8,16,1]{3,2,1,0:T(8,128)}, f32[2,8,16,1]{3,2,1,0:T(8,128)}, u32[]{:S(2)}, u32[]{:S(2)}) collective-permute-start(f32[2,8,16,1]{3,2,1,0:T(8,128)} %get-tuple-element.40), channel_id=1, source_target_pairs={{1,0},{2,1},{3,2},{0,3},{5,4},{6,5},{7,6},{4,7},{9,8},{10,9},{11,1... | collective-permute-start | bytes 3080 | tf_op jit(solution)/shard_map/ppermute | solution.py:24
  245.5 28.5 %collective-permute-start.30 = (f32[2,8,16,1]{3,2,1,0:T(8,128)S(1)}, f32[2,8,16,1]{3,2,1,0:T(8,128)}, u32[]{:S(2)}, u32[]{:S(2)}) collective-permute-start(f32[2,8,16,1]{3,2,1,0:T(8,128)S(1)} %get-tuple-element.39), channel_id=1, source_target_pairs={{0,1},{1,2},{2,3},{3,0},{4,5},{5,6},{6,7},{7,4},{8,9},{9,10},{10,1... | collective-permute-start | bytes 3080 | tf_op jit(solution)/shard_map/ppermute | solution.py:21
  248.8 31.1 %collective-permute-start.29 = (f32[2,8,1,64]{3,2,1,0:T(1,128)}, f32[2,8,1,64]{3,2,1,0:T(1,128)S(1)}, u32[]{:S(2)}, u32[]{:S(2)}) collective-permute-start(f32[2,8,1,64]{3,2,1,0:T(1,128)} %get-tuple-element.38), channel_id=1, source_target_pairs={{4,0},{8,4},{12,8},{16,12},{20,16},{24,20},{28,24},{5,1},{9,5},{13... | collective-permute-start | bytes 12296 | tf_op jit(solution)/shard_map/ppermute | solution.py:24
  255.2 28.5 %collective-permute-start.28 = (f32[2,8,1,64]{3,2,1,0:T(1,128)}, f32[2,8,1,64]{3,2,1,0:T(1,128)}, u32[]{:S(2)}, u32[]{:S(2)}) collective-permute-start(f32[2,8,1,64]{3,2,1,0:T(1,128)} %get-tuple-element.37), channel_id=1, source_target_pairs={{0,4},{4,8},{8,12},{12,16},{16,20},{20,24},{24,28},{1,5},{5,9},{9,... | collective-permute-start | bytes 12296 | tf_op jit(solution)/shard_map/ppermute | solution.py:21
  263.8 27.8 %collective-permute-start.15 = (f32[2,8,32,1]{2,1,3,0:T(8,128)}, f32[2,8,32,1]{2,1,3,0:T(8,128)S(1)}, u32[]{:S(2)}, u32[]{:S(2)}) collective-permute-start(f32[2,8,32,1]{2,1,3,0:T(8,128)} %get-tuple-element.8), channel_id=1, source_target_pairs={{1,0},{2,1},{3,2},{0,3},{5,4},{6,5},{7,6},{4,7},{9,8},{10,9},{11,1... | collective-permute-start | bytes 6152 | tf_op jit(solution)/shard_map/ppermute | solution.py:24
  272.0 19.5 %collective-permute-start.14 = (f32[2,8,32,1]{2,1,3,0:T(8,128)}, f32[2,8,32,1]{2,1,3,0:T(8,128)}, u32[]{:S(2)}, u32[]{:S(2)}) collective-permute-start(f32[2,8,32,1]{2,1,3,0:T(8,128)} %get-tuple-element.7), channel_id=1, source_target_pairs={{0,1},{1,2},{2,3},{3,0},{4,5},{5,6},{6,7},{7,4},{8,9},{9,10},{10,1... | collective-permute-start | bytes 6152 | tf_op jit(solution)/shard_map/ppermute | solution.py:21
  273.9 12.1 %collective-permute-start.13 = (f32[2,8,1,128]{3,1,2,0:T(8,128)}, f32[2,8,1,128]{3,1,2,0:T(8,128)}, u32[]{:S(2)}, u32[]{:S(2)}) collective-permute-start(f32[2,8,1,128]{3,1,2,0:T(8,128)} %copy.362), channel_id=1, source_target_pairs={{4,0},{8,4},{12,8},{16,12},{20,16},{24,20},{28,24},{5,1},{9,5},{13... | collective-permute-start | bytes 24584 | tf_op jit(solution)/shard_map/ppermute | solution.py:24
  279.9 9.5 %collective-permute-start.12 = (f32[2,8,1,128]{3,1,2,0:T(8,128)}, f32[2,8,1,128]{3,1,2,0:T(8,128)}, u32[]{:S(2)}, u32[]{:S(2)}) collective-permute-start(f32[2,8,1,128]{3,1,2,0:T(8,128)} %copy.360), channel_id=1, source_target_pairs={{0,4},{4,8},{8,12},{12,16},{16,20},{20,24},{24,28},{1,5},{5,9},{9,... | collective-permute-start | bytes 24584 | tf_op jit(solution)/shard_map/ppermute | solution.py:21
  (9 other events, 103.3 us)
Sparse Core Ops, SparseCore 0:
  297.9 127.5 all-reduce.1
where the time goes:
time: 437 us; the launch traced here: 434 us
  starting transfers between devices  197 us (45%)
  waiting for transfers between devices  139 us (32%)
  local copies, waits for them, and re-layouts  54.8 us (13%)
  other arithmetic  29 us (7%)
  between operations  14.3 us (3%)
    ppermute x24, starting transfers between devices, with_halo(): lax.ppermute(lax.slice_in_dim(block, 0, width, axis=dim), axis, backward)  129 us
    psum x1, waiting for transfers between devices, body(): summed = lax.psum(partial_value, 'mem')  128 us
    ppermute x24, starting transfers between devices, with_halo(): lax.ppermute(lax.slice_in_dim(block, block.shape[dim] - width, None, axis...  68.5 us
    slice x28, local copies, waits for them, and re-layouts, with_halo(): lax.slice_in_dim(block, block.shape[dim] - width, None, axis=dim)  19.6 us
    div x11, other arithmetic, diffuse_single(): smoothed = (source + stiffness * beside_all) / (1.0 + 4.0 * stiffness)  14.9 us
    ppermute x24, waiting for transfers between devices, with_halo(): lax.ppermute(lax.slice_in_dim(block, block.shape[dim] - width, None, axis...  11.1 us
    reduce_sum x2, other arithmetic, coarsen(): return jnp.mean(blocks, axis=(-3, -1))  9.21 us
  transfers between devices with their start and end apart: 49, of which 4 were waited for; matrix products, arithmetic and copies ran while one was open for 13% of the time, Pallas kernels for 0%

commit v1 on v0

v1 whole, which is shorter than its diff:
```python
import functools

import jax
import jax.numpy as jnp
from jax import lax
from jax.experimental import pallas as pl
from jax.experimental.pallas import tpu as pltpu
from jax.sharding import PartitionSpec as P

ITERS = 4
factors = (1, 2, 4)
stiffnesses = (1.0, 2.0, 4.0)
weights = (0.5, 0.3, 0.2)
scales = tuple(w / (1.0 + 4.0 * k) for w, k in zip(weights, stiffnesses))

LEV = 8
ROWS = 32
LANES = 128
PLANES = 16
MAIN = 8
CORNERS = 2


def lane_ids():
    return lax.broadcasted_iota(jnp.int32, (PLANES, LANES), 1)


def in_range(lane, start, width):
    return ((lane - start) & (LANES - 1)) < width


def pack_kernel(members_ref, increment_ref, held_ref, s1_ref, s2_ref, s4_ref, lon_ref, lat_ref, wide_ref):
    lane = lane_ids()
    here, count = lax.axis_index("lon"), lax.axis_size("lon")
    odd = lax.rem(lax.axis_index("lat"), 2)
    wide_ref[...] = members_ref[...].astype(jnp.float32)
    for row in range(ROWS):
        inc = increment_ref[pl.ds(row, LEV, stride=ROWS), :] * scales[0]
        for m in range(2):
            value = wide_ref[pl.ds(m * LEV * ROWS + row, LEV, stride=ROWS), :]
            held_ref[row, m * LEV : (m + 1) * LEV, :] = value
            s1_ref[row, m * LEV : (m + 1) * LEV, :] = value * inc
    for row in range(ROWS // 2):
        pair = s1_ref[2 * row] + s1_ref[2 * row + 1]
        pair = pair + jnp.where((lane & 1) == 0, pltpu.roll(pair, LANES - 1, 1), pltpu.roll(pair, 1, 1))
        s2_ref[row] = pair * (0.25 * scales[1] / scales[0])
    for row in range(ROWS // 4):
        pair = s2_ref[2 * row] + s2_ref[2 * row + 1]
        pair = pair + jnp.where((lane & 2) == 0, pltpu.roll(pair, LANES - 2, 1), pltpu.roll(pair, 2, 1))
        s4_ref[row] = pair * (0.25 * scales[2] / scales[1])

    tiles = []
    for ref, factor in ((s1_ref, 1), (s2_ref, 2), (s4_ref, 4)):
        width = ITERS * factor
        first = last = jnp.zeros((PLANES, LANES), jnp.float32)
        for row in range(ROWS // factor):
            turned = pltpu.roll(ref[row], width * row, 1) if row else ref[row]
            first = jnp.where(in_range(lane, width * row, width), turned, first)
            last = jnp.where(in_range(lane, width * row - width, width), turned, last)
        tiles.append((first, last))
    even = (lane & 1) == 0
    blank = jnp.zeros((2, PLANES, LANES), jnp.float32)
    lon_ref[here] = blank
    lon_ref[lax.rem(here + 2, count)] = blank
    for side, to in ((0, lax.rem(here + count - 1, count)), (1, lax.rem(here + 1, count))):
        lon_ref[to, 0] = tiles[0][side]
        lon_ref[to, 1] = jnp.where(even, tiles[1][side], tiles[2][side])

    for slot, tail in ((odd, True), (1 - odd, False)):
        for k in range(ITERS):
            at = lambda ref: ref[ref.shape[0] - ITERS + k] if tail else ref[k]
            lat_ref[slot, k] = at(s1_ref)
            lat_ref[slot, ITERS + k] = jnp.where(even, at(s2_ref), at(s4_ref))


def side_tiles(got_ref, lane):
    here, count = lax.axis_index("lon"), lax.axis_size("lon")
    even = (lane & 1) == 0
    out = []
    for of in (lax.rem(here + 1, count), lax.rem(here + count - 1, count)):
        mixed = got_ref[of, 1]
        out.append(
            (
                got_ref[of, 0],
                jnp.where(even, mixed, pltpu.roll(mixed, 1, 1)),
                jnp.where(even, pltpu.roll(mixed, LANES - 1, 1), mixed),
            )
        )
    return out


def beside(right, left, lane, width, row):
    both = jnp.where(in_range(lane, width * row, LANES // 2), right, left)
    return pltpu.roll(both, (LANES - width * row) % LANES, 1)


CORNER_PLACES = ((2, 0, 0, 16), (2, 1, 64, 16), (1, 0, 24, 8), (1, 1, 88, 8), (0, 0, 36, 4), (0, 1, 100, 4))


def corner_kernel(got_ref, lat_ref, out0_ref, out1_ref):
    lane = lane_ids()
    odd = lax.rem(lax.axis_index("lat"), 2)
    right, left = side_tiles(got_ref, lane)
    out0_ref[:MAIN] = lat_ref[0]
    out1_ref[:MAIN] = lat_ref[1]
    made = []
    for tail in (True, False):
        tiles = []
        for t in range(CORNERS):
            tile = jnp.zeros((PLANES, LANES), jnp.float32)
            for band, which, shift, width in CORNER_PLACES:
                row = 2 * t + which + (ROWS // factors[band] - ITERS if tail else 0)
                halo = beside(right[band], left[band], lane, width, row)
                halo = pltpu.roll(halo, shift, 1) if shift else halo
                tile = jnp.where(in_range(lane, shift - width, 2 * width), halo, tile)
            tiles.append(tile)
        made.append(tiles)
    is_odd = (lane * 0 + odd) == 1
    for t in range(CORNERS):
        tail, head = made[0][t], made[1][t]
        out0_ref[MAIN + t] = jnp.where(is_odd, head, tail)
        out1_ref[MAIN + t] = jnp.where(is_odd, tail, head)


def diffuse_kernel(held_ref, s1_ref, s2_ref, s4_ref, got_ref, lat0_ref, lat1_ref, out_ref, edge_ref, *scratch):
    lane = lane_ids()
    place, places = lax.axis_index("lat"), lax.axis_size("lat")
    odd = lax.rem(place, 2)
    right, left = side_tiles(got_ref, lane)
    edge_ref[0] = lat0_ref[...]
    edge_ref[1] = lat1_ref[...]
    even = (lane & 1) == 0
    above, below = edge_ref.at[1 - odd], edge_ref.at[odd]
    keep_above = jnp.where(place > 0, 1.0, 0.0).astype(jnp.float32)
    keep_below = jnp.where(place < places - 1, 1.0, 0.0).astype(jnp.float32)

    for band, (factor, stiffness) in enumerate(zip(factors, stiffnesses)):
        source, field = scratch[2 * band], scratch[2 * band + 1]
        own, rows, width = (s1_ref, s2_ref, s4_ref)[band], ROWS // factor, ITERS * factor
        for row in range(rows):
            source[ITERS + row, 0] = own[row]
            source[ITERS + row, 1] = beside(right[band], left[band], lane, width, row)
        for base, edge in ((0, above), (ITERS + rows, below)):
            for k in range(ITERS):
                if band == 0:
                    value = edge[k]
                else:
                    value = edge[ITERS + k]
                    turned = pltpu.roll(value, 1 if band == 1 else LANES - 1, 1)
                    value = jnp.where(even, value, turned) if band == 1 else jnp.where(even, turned, value)
                source[base + k, 0] = value
                shift = next(s for b, w, s, _ in CORNER_PLACES if b == band and w == k % 2)
                corner = edge[MAIN + k // 2]
                source[base + k, 1] = pltpu.roll(corner, LANES - shift, 1) if shift else corner
        low, high = lane < factor, lane >= LANES - factor
        for sweep in range(1, ITERS + 1):
            old = source if sweep == 1 else field
            gain = stiffness if sweep == 1 else stiffness / (1.0 + 4.0 * stiffness)
            start, stop = sweep, rows + 2 * ITERS - sweep
            halves = (0,) if sweep == ITERS else (0, 1)
            before = [old[start - 1, h] for h in halves]
            now = [old[start, 0], old[start, 1]]
            for row in range(start, stop):
                after = [old[row + 1, 0], old[row + 1, 1]]
                up = [pltpu.roll(v, factor, 1) for v in now]
                down = [pltpu.roll(v, LANES - factor, 1) for v in now]
                for h in halves:
                    total = before[h] + after[h]
                    total = total + jnp.where(low, up[1 - h], up[h])
                    total = total + jnp.where(high, down[1 - h], down[h])
                    value = source[row, h] + gain * total
                    if row < ITERS:
                        value = value * keep_above
                    elif row >= ITERS + rows:
                        value = value * keep_below
                    field[row, h] = value
                before, now = now, after
    for row in range(ROWS):
        total = scratch[1][ITERS + row, 0] + scratch[3][ITERS + row // 2, 0] + scratch[5][ITERS + row // 4, 0]
        total = total * held_ref[row]
        out_ref[pl.ds(row, LEV, stride=ROWS), :] = total[:LEV] + total[LEV:]


def tiles_of(*dims):
    return jax.ShapeDtypeStruct(dims + (PLANES, LANES), jnp.float32)


def vmem(count):
    return [pl.BlockSpec(memory_space=pltpu.VMEM)] * count


def body(members, increment):
    columns = lax.axis_size("lon")
    parts = lax.axis_size("mem")
    rows_of = lax.axis_size("lat")
    held, s1, s2, s4, to_lon, to_lat = pl.pallas_call(
        pack_kernel,
        out_shape=(
            tiles_of(ROWS),
            tiles_of(ROWS),
            tiles_of(ROWS // 2),
            tiles_of(ROWS // 4),
            tiles_of(columns, 2),
            tiles_of(2, MAIN),
        ),
        in_specs=vmem(2),
        out_specs=tuple(vmem(6)),
        scratch_shapes=[pltpu.VMEM((2 * LEV * ROWS, LANES), jnp.float32)],
        name="pack",
    )(members.reshape(2 * LEV * ROWS, LANES), increment.reshape(LEV * ROWS, LANES))
    from_lon = lax.all_to_all(to_lon, "lon", 0, 0)
    out0, out1 = pl.pallas_call(
        corner_kernel,
        out_shape=(tiles_of(MAIN + CORNERS), tiles_of(MAIN + CORNERS)),
        in_specs=vmem(2),
        out_specs=tuple(vmem(2)),
        name="corner",
    )(from_lon, to_lat)
    swap0 = [(i, i ^ 1) for i in range(rows_of)]
    swap1 = [(i, ((i + 1) ^ 1) - 1) for i in range(1, rows_of - 1)]
    in0 = lax.ppermute(out0, "lat", swap0)
    in1 = lax.ppermute(out1, "lat", swap1)
    fields = []
    for factor in factors:
        fields += [pltpu.VMEM((ROWS // factor + 2 * ITERS, 2, PLANES, LANES), jnp.float32)] * 2
    partial_value = pl.pallas_call(
        diffuse_kernel,
        out_shape=jax.ShapeDtypeStruct((LEV * ROWS, LANES), jnp.float32),
        in_specs=vmem(7),
        out_specs=vmem(1)[0],
        scratch_shapes=[pltpu.VMEM((2, MAIN + CORNERS, PLANES, LANES), jnp.float32)] + fields,
        name="diffuse",
    )(held, s1, s2, s4, from_lon, in0, in1)
    member_count = members.shape[0] * parts
    chunk = (parts, LEV * ROWS // parts, LANES)
    mine = jnp.sum(lax.all_to_all(partial_value.reshape(chunk), "mem", 0, 0), axis=0)
    mine = mine * (1.0 / (member_count - 1))
    whole = lax.all_to_all(jnp.broadcast_to(mine[None], chunk), "mem", 0, 0)
    return whole.reshape(LEV, ROWS, LANES)


def solution(mesh):
    return jax.shard_map(
        body,
        mesh=mesh,
        in_specs=(P("mem", None, "lat", "lon"), P(None, "lat", "lon")),
        out_specs=P(None, "lat", "lon"),
        check_vma=False,
    )
```

time: 437 us -> 71.8 us (0.16)
  starting transfers between devices: 197 us -> 10.1 us
  waiting for transfers between devices: 139 us -> 8 us
  local copies, waits for them, and re-layouts: 54.8 us -> 1.3 us
  blocking collectives: 0 us -> 43.2 us
  other arithmetic: 29 us -> 0.02 us
  between operations: 14.3 us -> 0.06 us
  Pallas kernels: 0 us -> 8.66 us
    ppermute x48 -> x2, starting transfers between devices: 197 us -> 10.1 us  [the longest x1 7.93 us: body(): in0 = lax.ppermute(out0, 'lat', swap0)]
    psum x1 -> x0, waiting for transfers between devices: 128 us -> none  [body(): summed = lax.psum(partial_value, 'mem')]
    all_to_all x0 -> x3, blocking collectives: none -> 43.2 us  [the longest x1 20 us: body(): lax.all_to_all(partial_value.reshape(chunk), 'mem', 0, 0)]
    slice x32 -> x0, local copies, waits for them, and re-layouts: 28.2 us -> none  [the longest x28 19.6 us: with_halo(): lax.slice_in_dim(block, block.shape[dim] - width, None, axis=dim)]
    div x14 -> x0, other arithmetic: 16.6 us -> none  [the longest x11 14.9 us: diffuse_single(): smoothed = (source + stiffness * beside_all) / (1.0 + 4.0 * stiffness)]
    reduce_sum x3 -> x1, other arithmetic: 12.4 us -> 0.02 us  [body(): jnp.sum(lax.all_to_all(partial_value.reshape(chunk), 'mem', 0, 0), axis=0)]
    ppermute x8 -> x0, local copies, waits for them, and re-layouts: 11.5 us -> none  [the longest x4 6.18 us: with_halo(): lax.ppermute(lax.slice_in_dim(block, block.shape[dim] - width, None, axis...]
    pallas_call x0 -> x3, Pallas kernels: none -> 8.66 us  [the longest x1 4.52 us: body(): pl.pallas_call(diffuse_kernel, out_shape=jax.ShapeDtypeStruct((LEV * ROWS...]
  transfers between devices with their start and end apart: 49 -> 2, of which waited for: 4 -> 1; matrix products, arithmetic and copies ran while one was open for 13% -> 0% of each run, Pallas kernels for 0% -> 0%
where the time goes in v1:
time: 71.8 us; the launch traced here: 71.4 us
  blocking collectives  43.2 us (60%)
  starting transfers between devices  10.1 us (14%)
  Pallas kernels  8.66 us (12%)
  waiting for transfers between devices  8 us (11%)
  local copies, waits for them, and re-layouts  1.3 us (2%)
    all_to_all x1, blocking collectives, body(): lax.all_to_all(partial_value.reshape(chunk), 'mem', 0, 0)  20 us
    all_to_all x1, blocking collectives, body(): from_lon = lax.all_to_all(to_lon, 'lon', 0, 0)  11.7 us
    all_to_all x1, blocking collectives, body(): whole = lax.all_to_all(jnp.broadcast_to(mine[None], chunk), 'mem', 0, 0)  11.6 us
    ppermute x1, waiting for transfers between devices, body(): in1 = lax.ppermute(out1, 'lat', swap1)  8 us
    ppermute x1, starting transfers between devices, body(): in0 = lax.ppermute(out0, 'lat', swap0)  7.93 us
    pallas_call x1, Pallas kernels, body(): pl.pallas_call(diffuse_kernel, out_shape=jax.ShapeDtypeStruct((LEV * ROWS...  4.52 us
    pallas_call x1, Pallas kernels, body(): pl.pallas_call(pack_kernel, out_shape=(tiles_of(ROWS), tiles_of(ROWS), ti...  2.29 us
    ppermute x1, starting transfers between devices, body(): in1 = lax.ppermute(out1, 'lat', swap1)  2.19 us
  transfers between devices with their start and end apart: 2, of which 1 were waited for; matrix products, arithmetic and copies ran while one was open for 0% of the time, Pallas kernels for 0%

profile of v1, /device:TPU:7, one launch (start us, length us, event | category | flops | bytes accessed | tf_op | source)
XLA Modules:
  0.0 71.4 jit_solution(17296026204231609310)
XLA Ops:
  0.0 2.3 %pack.1 = (f32[32,16,128]{2,1,0:T(8,128)}, f32[32,16,128]{2,1,0:T(8,128)}, f32[16,16,128]{2,1,0:T(8,128)}, f32[8,16,128]{2,1,0:T(8,128)}, f32[4,2,16,128]{3,2,1,0:T(8,128)}, /*index=5*/f32[2,8,16,128]{3,2,1,0:T(8,128)}) custom-call(bf16[512,128]{1,0:T(8,128)(2,1)} %bitcast.6, f32[256,128]{1,0:T(8,128)} %bitcast.7), custom_call_target="tpu_custom_call" | custom-call | tf_op jit(solution)/shard_map/pack/pallas_call | solution.py:196
  2.3 11.7 %all_to_all.15.got_ref = f32[4,2,16,128]{3,2,1,0:T(8,128)} all-to-all(f32[4,2,16,128]{3,2,1,0:T(8,128)} %get-tuple-element.17), channel_id=1, replica_groups=mesh['mem'=16,'lat'=8,'lon'=4] {'lon'}, dimensions={0} | all-to-all | bytes 131072 | tf_op jit(solution)/shard_map/all_to_all | solution.py:211
  14.0 1.9 %corner.1 = (f32[10,16,128]{2,1,0:T(8,128)}, f32[10,16,128]{2,1,0:T(8,128)}) custom-call(f32[4,2,16,128]{3,2,1,0:T(8,128)} %all_to_all.15.got_ref, f32[2,8,16,128]{3,2,1,0:T(8,128)} %get-tuple-element.18.lat_ref), custom_call_target="tpu_custom_call" | custom-call | tf_op jit(solution)/shard_map/corner/pallas_call | solution.py:212
  15.8 7.9 %collective-permute-start = (f32[10,16,128]{2,1,0:T(8,128)}, f32[10,16,128]{2,1,0:T(8,128)S(1)}, u32[]{:S(2)}, u32[]{:S(2)}) collective-permute-start(f32[10,16,128]{2,1,0:T(8,128)} %get-tuple-element.19), channel_id=1, source_target_pairs={{0,4},{4,0},{8,12},{12,8},{16,20},{20,16},{24,28},{28,24},{1,5},{5... | collective-permute-start | bytes 245768 | tf_op jit(solution)/shard_map/ppermute | solution.py:221
  23.8 2.2 %collective-permute-start.1 = (f32[10,16,128]{2,1,0:T(8,128)}, f32[10,16,128]{2,1,0:T(8,128)S(1)}, u32[]{:S(2)}, u32[]{:S(2)}) collective-permute-start(f32[10,16,128]{2,1,0:T(8,128)} %get-tuple-element.20), channel_id=1, source_target_pairs={{4,8},{8,4},{12,16},{16,12},{20,24},{24,20},{5,9},{9,5},{13,17},{1... | collective-permute-start | bytes 245768 | tf_op jit(solution)/shard_map/ppermute | solution.py:222
  26.0 0.0 collective-permute-done.lat0_ref
  26.0 0.0 copy-start
  26.0 8.0 %collective-permute-done.1.lat1_ref = f32[10,16,128]{2,1,0:T(8,128)S(1)} collective-permute-done((f32[10,16,128]{2,1,0:T(8,128)}, f32[10,16,128]{2,1,0:T(8,128)S(1)}, u32[]{:S(2)}, u32[]{:S(2)}) %collective-permute-start.1) | collective-permute-done | bytes 81952 | tf_op jit(solution)/shard_map/ppermute | solution.py:222
  34.0 0.0 copy-start.1
  34.0 0.0 copy-done
  34.0 0.6 copy-done.1
  34.6 4.5 %diffuse.1 = f32[256,128]{1,0:T(8,128)} custom-call(f32[32,16,128]{2,1,0:T(8,128)} %get-tuple-element.13.held_ref, f32[32,16,128]{2,1,0:T(8,128)} %get-tuple-element.14.s1_ref, f32[16,16,128]{2,1,0:T(8,128)} %get-tuple-element.15.s2_ref, f32[8,16,128]{2,1,0:T(8,128)} %get-tuple-element.16.s4_ref, f32[4,2,16,128]{3,2,1,0:T(8,128)} %all_to_all.15.got_ref, ...), custom_call_target="tpu_custom_call" | custom-call | tf_op jit(solution)/shard_map/diffuse/pallas_call | solution.py:226
  39.1 20.0 %all_to_all.16 = f32[16,16,128]{2,1,0:T(8,128)S(1)} all-to-all(f32[16,16,128]{2,1,0:T(8,128)} %bitcast.4), channel_id=1, replica_groups=mesh['mem'=16,'lat'=8,'lon'=4] {'mem'}, dimensions={0} | all-to-all | bytes 262144 | tf_op jit(solution)/shard_map/all_to_all | solution.py:236
  59.2 11.6 %all_to_all.17 = f32[16,16,128]{2,1,0:T(8,128)S(1)} all-to-all(f32[16,16,128]{2,1,0:T(8,128)S(1)} %broadcast_in_dim.2), channel_id=1, replica_groups=mesh['mem'=16,'lat'=8,'lon'=4] {'mem'}, dimensions={0} | all-to-all | bytes 262144 | tf_op jit(solution)/shard_map/all_to_all | solution.py:238
  70.7 0.7 copy.4
  (3 shorter events, 0.0 us)
Async XLA Ops:
  15.8 10.1 %collective-permute-start = (f32[10,16,128]{2,1,0:T(8,128)}, f32[10,16,128]{2,1,0:T(8,128)S(1)}, u32[]{:S(2)}, u32[]{:S(2)}) collective-permute-start(f32[10,16,128]{2,1,0:T(8,128)} %get-tuple-element.19), channel_id=1, source_target_pairs={{0,4},{4,0},{8,12},{12,8},{16,20},{20,16},{24,28},{28,24},{1,5},{5... | collective-permute-start | bytes 245768 | tf_op jit(solution)/shard_map/ppermute | solution.py:221
  23.8 10.2 %collective-permute-start.1 = (f32[10,16,128]{2,1,0:T(8,128)}, f32[10,16,128]{2,1,0:T(8,128)S(1)}, u32[]{:S(2)}, u32[]{:S(2)}) collective-permute-start(f32[10,16,128]{2,1,0:T(8,128)} %get-tuple-element.20), channel_id=1, source_target_pairs={{4,8},{8,4},{12,16},{16,12},{20,24},{24,20},{5,9},{9,5},{13,17},{1... | collective-permute-start | bytes 245768 | tf_op jit(solution)/shard_map/ppermute | solution.py:222
  26.0 8.0 %copy-start = (f32[10,16,128]{2,1,0:T(8,128)}, f32[10,16,128]{2,1,0:T(8,128)S(1)}, u32[]{:S(2)}) copy-start(f32[10,16,128]{2,1,0:T(8,128)S(1)} %collective-permute-done.lat0_ref) | copy-start | bytes 245764
  34.0 0.6 copy-start.1

commit v2 on v1

v2 whole, which is shorter than its diff:
```python
import functools

import jax
import jax.numpy as jnp
from jax import lax
from jax.experimental import pallas as pl
from jax.experimental.pallas import tpu as pltpu
from jax.sharding import PartitionSpec as P

ITERS = 4
factors = (1, 2, 4)
stiffnesses = (1.0, 2.0, 4.0)
weights = (0.5, 0.3, 0.2)
scales = tuple(w / (1.0 + 4.0 * k) for w, k in zip(weights, stiffnesses))

LEV = 8
ROWS = 32
LANES = 128
PLANES = 16
GRANT = 16 * 1024 * 1024
EDGE = 9
CORNER = EDGE - 1


def lane_ids():
    return lax.broadcasted_iota(jnp.int32, (PLANES, LANES), 1)


def in_range(lane, start, width):
    return ((lane - start) & (LANES - 1)) < width


def pack_kernel(
    members_hbm, increment_hbm, held_ref, s1_ref, s2_ref, s4_ref, lon_ref, lat_ref, members_ref, increment_ref, wide_ref, sems
):
    lane = lane_ids()
    here, count = lax.axis_index("lon"), lax.axis_size("lon")
    odd = lax.rem(lax.axis_index("lat"), 2)
    half = LEV * ROWS
    fetches = [pltpu.make_async_copy(increment_hbm, increment_ref, sems.at[0])]
    for m in range(2):
        part = pl.ds(m * half, half)
        fetches.append(pltpu.make_async_copy(members_hbm.at[part], members_ref.at[part], sems.at[1 + m]))
    for fetch in fetches:
        fetch.start()
    fetches[0].wait()
    for m in range(2):
        fetches[1 + m].wait()
        wide_ref[m * half : (m + 1) * half] = members_ref[m * half : (m + 1) * half].astype(jnp.float32)
        for row in range(ROWS):
            inc = increment_ref[pl.ds(row, LEV, stride=ROWS), :] * scales[0]
            value = wide_ref[pl.ds(m * half + row, LEV, stride=ROWS), :]
            held_ref[row, m * LEV : (m + 1) * LEV, :] = value
            s1_ref[row, m * LEV : (m + 1) * LEV, :] = value * inc
    for row in range(ROWS // 2):
        pair = s1_ref[2 * row] + s1_ref[2 * row + 1]
        pair = pair + jnp.where((lane & 1) == 0, pltpu.roll(pair, LANES - 1, 1), pltpu.roll(pair, 1, 1))
        s2_ref[row] = pair * (0.25 * scales[1] / scales[0])
    for row in range(ROWS // 4):
        pair = s2_ref[2 * row] + s2_ref[2 * row + 1]
        pair = pair + jnp.where((lane & 2) == 0, pltpu.roll(pair, LANES - 2, 1), pltpu.roll(pair, 2, 1))
        s4_ref[row] = pair * (0.25 * scales[2] / scales[1])

    tiles = []
    for ref, factor in ((s1_ref, 1), (s2_ref, 2), (s4_ref, 4)):
        width = ITERS * factor
        first = last = jnp.zeros((PLANES, LANES), jnp.float32)
        for row in range(ROWS // factor):
            turned = pltpu.roll(ref[row], width * row, 1) if row else ref[row]
            first = jnp.where(in_range(lane, width * row, width), turned, first)
            last = jnp.where(in_range(lane, width * row - width, width), turned, last)
        tiles.append((first, last))
    even = (lane & 1) == 0
    blank = jnp.zeros((2, PLANES, LANES), jnp.float32)
    lon_ref[here] = blank
    lon_ref[lax.rem(here + 2, count)] = blank
    for side, to in ((0, lax.rem(here + count - 1, count)), (1, lax.rem(here + 1, count))):
        lon_ref[to, 0] = tiles[0][side]
        lon_ref[to, 1] = jnp.where(even, tiles[1][side], tiles[2][side])

    for slot, tail in ((odd, True), (1 - odd, False)):
        for k in range(ITERS):
            at = lambda ref: ref[ref.shape[0] - ITERS + k] if tail else ref[k]
            lat_ref[slot, k] = at(s1_ref)
            lat_ref[slot, ITERS + k] = jnp.where(even, at(s2_ref), at(s4_ref))


def side_tiles(got_ref, lane):
    here, count = lax.axis_index("lon"), lax.axis_size("lon")
    even = (lane & 1) == 0
    out = []
    for of in (lax.rem(here + 1, count), lax.rem(here + count - 1, count)):
        mixed = got_ref[of, 1]
        out.append(
            (
                got_ref[of, 0],
                jnp.where(even, mixed, pltpu.roll(mixed, 1, 1)),
                jnp.where(even, pltpu.roll(mixed, LANES - 1, 1), mixed),
            )
        )
    return out


def beside(right, left, lane, width, row):
    both = jnp.where(in_range(lane, width * row, LANES // 2), right, left)
    return pltpu.roll(both, (LANES - width * row) % LANES, 1)


CORNER_PLACES = ((2, 1, 0), (2, 2, 20), (2, 3, 32), (1, 1, 42), (1, 2, 52), (1, 3, 58), (0, 1, 63), (0, 2, 68), (0, 3, 71))
SHIFTS = {(band, distance): shift for band, distance, shift in CORNER_PLACES}


def corner_kernel(got_ref, lat_ref, out0_ref, out1_ref):
    lane = lane_ids()
    odd = lax.rem(lax.axis_index("lat"), 2)
    right, left = side_tiles(got_ref, lane)
    out0_ref[:CORNER] = lat_ref[0]
    out1_ref[:CORNER] = lat_ref[1]
    made = []
    for tail in (True, False):
        tile = jnp.zeros((PLANES, LANES), jnp.float32)
        for band, distance, shift in CORNER_PLACES:
            factor = factors[band]
            width = factor * (ITERS - distance)
            row = ROWS // factor - distance if tail else distance - 1
            halo = beside(right[band], left[band], lane, ITERS * factor, row)
            halo = pltpu.roll(halo, shift, 1) if shift else halo
            tile = jnp.where(in_range(lane, shift - width, 2 * width), halo, tile)
        made.append(tile)
    is_odd = (lane * 0 + odd) == 1
    out0_ref[CORNER] = jnp.where(is_odd, made[1], made[0])
    out1_ref[CORNER] = jnp.where(is_odd, made[0], made[1])


def sweep_row(before, now, after, base, factor, gain, lane, halves=(0, 1)):
    low, high = lane < factor, lane >= LANES - factor
    up = [pltpu.roll(v, factor, 1) for v in now]
    down = [pltpu.roll(v, LANES - factor, 1) for v in now]
    out = []
    for h in halves:
        total = before[h] + after[h]
        total = total + jnp.where(low, up[1 - h], up[h])
        total = total + jnp.where(high, down[1 - h], down[h])
        out.append(base[h] + gain * total)
    return out


def gain_of(stiffness, sweep):
    return stiffness if sweep == 1 else stiffness / (1.0 + 4.0 * stiffness)


def inner_kernel(s1_ref, s2_ref, s4_ref, got_ref, *levels):
    lane = lane_ids()
    right, left = side_tiles(got_ref, lane)
    for band, (factor, stiffness) in enumerate(zip(factors, stiffnesses)):
        level, own, rows = levels[band], (s1_ref, s2_ref, s4_ref)[band], ROWS // factor
        for row in range(rows):
            level[0, row, 0] = own[row]
            level[0, row, 1] = beside(right[band], left[band], lane, ITERS * factor, row)
        for sweep in range(1, ITERS + 1):
            halves = (0,) if sweep == ITERS else (0, 1)
            load = lambda row: [level[sweep - 1, row, h] for h in (0, 1)]
            if rows - sweep <= sweep:
                continue
            before, now = load(sweep - 1), load(sweep)
            for row in range(sweep, rows - sweep):
                after = load(row + 1)
                base = [level[0, row, h] for h in halves]
                value = sweep_row(before, now, after, base, factor, gain_of(stiffness, sweep), lane, halves)
                for h in halves:
                    level[sweep, row, h] = value[h]
                before, now = now, after


def outer_kernel(held_ref, lat0_ref, lat1_ref, level1_ref, level2_ref, level4_ref, out_ref, edge_ref, ends_ref):
    lane = lane_ids()
    even = (lane & 1) == 0
    place, places = lax.axis_index("lat"), lax.axis_size("lat")
    odd = lax.rem(place, 2)
    edge_ref[0] = lat0_ref[...]
    edge_ref[1] = lat1_ref[...]
    found = []
    for band, (factor, stiffness) in enumerate(zip(factors, stiffnesses)):
        level, rows = (level1_ref, level2_ref, level4_ref)[band], ROWS // factor
        ends = {}
        for top in (True, False):
            edge = edge_ref.at[1 - odd] if top else edge_ref.at[odd]
            keep = jnp.where(place > 0 if top else place < places - 1, 1.0, 0.0).astype(jnp.float32)
            row_at = (lambda d: -d) if top else (lambda d: rows - 1 + d)
            outside = {}
            for distance in range(1, ITERS + 1):
                k = ITERS - distance if top else distance - 1
                if band == 0:
                    value = edge[k]
                else:
                    value = edge[ITERS + k]
                    turned = pltpu.roll(value, 1 if band == 1 else LANES - 1, 1)
                    value = jnp.where(even, value, turned) if band == 1 else jnp.where(even, turned, value)
                corner = edge[CORNER]
                shift = SHIFTS.get((band, distance), 0)
                outside[row_at(distance)] = [value, pltpu.roll(corner, LANES - shift, 1) if shift else corner]
            latest = dict(outside)
            for sweep in range(1, ITERS + 1):
                halves = (0,) if sweep == ITERS else (0, 1)

                def load(row):
                    return latest[row] if row in latest else [level[sweep - 1, row, h] for h in (0, 1)]

                new = {}
                for distance in range(1 - sweep, ITERS + 1 - sweep):
                    row = row_at(distance)
                    base = outside[row] if distance > 0 else [level[0, row, h] for h in halves]
                    value = sweep_row(
                        load(row - 1), load(row), load(row + 1), base, factor, gain_of(stiffness, sweep), lane, halves
                    )
                    new[row] = [v * keep for v in value] if distance > 0 else value
                latest = new
            for row in range(ITERS):
                at = row if top else ITERS + row
                ends_ref[band, at] = latest[row if top else rows - ITERS + row][0]
    def final(band, row):
        rows = ROWS // factors[band]
        if row < ITERS:
            return ends_ref[band, row]
        if row >= rows - ITERS:
            return ends_ref[band, row - rows + 2 * ITERS]
        return (level1_ref, level2_ref, level4_ref)[band][ITERS, row, 0]

    for row in range(ROWS):
        total = (final(0, row) + final(1, row // 2) + final(2, row // 4)) * held_ref[row]
        out_ref[pl.ds(row, LEV, stride=ROWS), :] = total[:LEV] + total[LEV:]


def tiles_of(*dims):
    return pltpu.VMEM(dims + (PLANES, LANES), jnp.float32)


def on_chip(kernel, name, out_shape, scratch_shapes=(), held_in=pltpu.VMEM, bundles=1000):
    several = isinstance(out_shape, tuple)
    spec = pl.BlockSpec(memory_space=pltpu.VMEM)

    def call(*operands):
        return pl.pallas_call(
            kernel,
            out_shape=out_shape,
            in_specs=[spec if held_in == pltpu.VMEM else pl.BlockSpec(memory_space=pl.ANY)] * len(operands),
            out_specs=(spec,) * len(out_shape) if several else spec,
            scratch_shapes=scratch_shapes,
            compiler_params=pltpu.CompilerParams(vmem_limit_bytes=GRANT),
            cost_estimate=pl.CostEstimate(flops=bundles * 4096, bytes_accessed=bundles * 1024, transcendentals=0),
            name=name,
        )(*[pltpu.with_memory_space_constraint(x, held_in) for x in operands])

    return call


def body(members, increment):
    columns = lax.axis_size("lon")
    parts = lax.axis_size("mem")
    rows_of = lax.axis_size("lat")
    held, s1, s2, s4, to_lon, to_lat = on_chip(
        pack_kernel,
        "pack",
        (
            tiles_of(ROWS),
            tiles_of(ROWS),
            tiles_of(ROWS // 2),
            tiles_of(ROWS // 4),
            tiles_of(columns, 2),
            tiles_of(2, CORNER),
        ),
        [
            pltpu.VMEM((2 * LEV * ROWS, LANES), jnp.bfloat16),
            pltpu.VMEM((LEV * ROWS, LANES), jnp.float32),
            pltpu.VMEM((2 * LEV * ROWS, LANES), jnp.float32),
            pltpu.SemaphoreType.DMA((3,)),
        ],
        held_in=pltpu.HBM,
    )(members.reshape(2 * LEV * ROWS, LANES), increment.reshape(LEV * ROWS, LANES))
    from_lon = lax.all_to_all(to_lon, "lon", 0, 0)
    out0, out1 = on_chip(corner_kernel, "corner", (tiles_of(EDGE), tiles_of(EDGE)))(from_lon, to_lat)
    swap0 = [(i, i ^ 1) for i in range(rows_of)]
    swap1 = [(i, ((i + 1) ^ 1) - 1) for i in range(1, rows_of - 1)]
    in0 = lax.ppermute(out0, "lat", swap0)
    in1 = lax.ppermute(out1, "lat", swap1)
    levels = on_chip(
        inner_kernel, "inner", tuple(tiles_of(ITERS + 1, ROWS // factor, 2) for factor in factors), bundles=3000
    )(s1, s2, s4, from_lon)
    partial_value = on_chip(
        outer_kernel,
        "outer",
        pltpu.VMEM((LEV * ROWS, LANES), jnp.float32),
        [tiles_of(2, EDGE), tiles_of(3, 2 * ITERS)],
    )(held, in0, in1, *levels)
    member_count = members.shape[0] * parts
    chunk = (parts, LEV * ROWS // parts, LANES)
    mine = jnp.sum(lax.all_to_all(partial_value.reshape(chunk), "mem", 0, 0), axis=0)
    mine = mine * (1.0 / (member_count - 1))
    whole = lax.all_to_all(jnp.broadcast_to(mine[None], chunk), "mem", 0, 0)
    return whole.reshape(LEV, ROWS, LANES)


def solution(mesh):
    return jax.shard_map(
        body,
        mesh=mesh,
        in_specs=(P("mem", None, "lat", "lon"), P(None, "lat", "lon")),
        out_specs=P(None, "lat", "lon"),
        check_vma=False,
    )
```

time: 71.8 us -> 64.5 us (0.90)
  Pallas kernels: 8.66 us -> 5.07 us
  blocking collectives: 43.2 us -> 41.2 us
  waiting for transfers between devices: 8 us -> 7.08 us
    pallas_call x3 -> x4, Pallas kernels: 8.66 us -> 5.07 us  [call(): pl.pallas_call(kernel, out_shape=out_shape, in_specs=[spec if held_in ==...]
    all_to_all x1, blocking collectives: 20 us -> 18.2 us  [body(): lax.all_to_all(partial_value.reshape(chunk), 'mem', 0, 0)]
    ppermute x1, waiting for transfers between devices: 8 us -> 7.07 us  [body(): in1 = lax.ppermute(out1, 'lat', swap1)]
  transfers between devices with their start and end apart: 2 -> 2, of which waited for: 1 -> 1; matrix products, arithmetic and copies ran while one was open for 0% -> 0% of each run, Pallas kernels for 0% -> 3%
where the time goes in v2:
time: 64.5 us; the launch traced here: 64.2 us
  blocking collectives  41.2 us (64%)
  starting transfers between devices  10.1 us (16%)
  waiting for transfers between devices  7.08 us (11%)
  Pallas kernels  5.07 us (8%)
  local copies, waits for them, and re-layouts  0.67 us (1%)
    all_to_all x1, blocking collectives, body(): lax.all_to_all(partial_value.reshape(chunk), 'mem', 0, 0)  18.2 us
    all_to_all x1, blocking collectives, body(): whole = lax.all_to_all(jnp.broadcast_to(mine[None], chunk), 'mem', 0, 0)  11.6 us
    all_to_all x1, blocking collectives, body(): from_lon = lax.all_to_all(to_lon, 'lon', 0, 0)  11.4 us
    ppermute x1, starting transfers between devices, body(): in0 = lax.ppermute(out0, 'lat', swap0)  7.94 us
    ppermute x1, waiting for transfers between devices, body(): in1 = lax.ppermute(out1, 'lat', swap1)  7.07 us
    pallas_call x4, Pallas kernels, call(): pl.pallas_call(kernel, out_shape=out_shape, in_specs=[spec if held_in ==...  5.07 us
    ppermute x1, starting transfers between devices, body(): in1 = lax.ppermute(out1, 'lat', swap1)  2.19 us
  transfers between devices with their start and end apart: 2, of which 1 were waited for; matrix products, arithmetic and copies ran while one was open for 0% of the time, Pallas kernels for 3%

profile of v2, /device:TPU:7, one launch (start us, length us, event | category | flops | bytes accessed | tf_op | source)
XLA Modules:
  0.0 64.2 jit_solution(15310808391199399699)
XLA Ops:
  0.0 1.5 %pack.1 = (f32[32,16,128]{2,1,0:T(8,128)S(1)}, f32[32,16,128]{2,1,0:T(8,128)S(1)}, f32[16,16,128]{2,1,0:T(8,128)S(1)}, f32[8,16,128]{2,1,0:T(8,128)S(1)}, f32[4,...) custom-call(bf16[512,128]{1,0:T(8,128)(2,1)} %bitcast.6, f32[256,128]{1,0:T(8,128)} %bitcast.7), custom_call_target="tpu_custom_call" | custom-call | flops 4096000 | bytes 1024000 | tf_op jit(solution)/shard_map/pack/pallas_call | solution.py:243
  1.6 11.4 %all_to_all.15.got_ref = f32[4,2,16,128]{3,2,1,0:T(8,128)S(1)} all-to-all(f32[4,2,16,128]{3,2,1,0:T(8,128)S(1)} %get-tuple-element.17), channel_id=1, replica_groups=mesh['mem'=16,'lat'=8,'lon'=4] {'lon'}, dimensions={0} | all-to-all | bytes 131072 | tf_op jit(solution)/shard_map/all_to_all | solution.py:280
  12.9 0.2 corner.1
  13.2 7.9 %collective-permute-start = (f32[9,16,128]{2,1,0:T(8,128)S(1)}, f32[9,16,128]{2,1,0:T(8,128)S(1)}, u32[]{:S(2)}, u32[]{:S(2)}) collective-permute-start(f32[9,16,128]{2,1,0:T(8,128)S(1)} %get-tuple-element.19), channel_id=1, source_target_pairs={{0,4},{4,0},{8,12},{12,8},{16,20},{20,16},{24,28},{28,24},{1,5},{5... | collective-permute-start | bytes 221192 | tf_op jit(solution)/shard_map/ppermute | solution.py:284
  21.1 2.2 %collective-permute-start.1 = (f32[9,16,128]{2,1,0:T(8,128)S(1)}, f32[9,16,128]{2,1,0:T(8,128)S(1)}, u32[]{:S(2)}, u32[]{:S(2)}) collective-permute-start(f32[9,16,128]{2,1,0:T(8,128)S(1)} %get-tuple-element.20), channel_id=1, source_target_pairs={{4,8},{8,4},{12,16},{16,12},{20,24},{24,20},{5,9},{9,5},{13,17},{1... | collective-permute-start | bytes 221192 | tf_op jit(solution)/shard_map/ppermute | solution.py:285
  23.3 1.7 %inner.1 = (f32[5,32,2,16,128]{4,3,2,1,0:T(8,128)S(1)}, f32[5,16,2,16,128]{4,3,2,1,0:T(8,128)S(1)}, f32[5,8,2,16,128]{4,3,2,1,0:T(8,128)S(1)}) custom-call(f32[32,16,128]{2,1,0:T(8,128)S(1)} %get-tuple-element.21.s1_ref, f32[16,16,128]{2,1,0:T(8,128)S(1)} %get-tuple-element.22.s2_ref, f32[8,16,128]{2,1,0:T(8,128)S(1)} %get-tuple-element.23.s4_ref, ...), custom_call_target="tpu_custom_call" | custom-call | flops 12288000 | bytes 3072000 | tf_op jit(solution)/shard_map/inner/pallas_call | solution.py:243
  25.0 0.0 collective-permute-done.lat0_ref
  25.0 7.1 %collective-permute-done.1.lat1_ref = f32[9,16,128]{2,1,0:T(8,128)S(1)} collective-permute-done((f32[9,16,128]{2,1,0:T(8,128)S(1)}, f32[9,16,128]{2,1,0:T(8,128)S(1)}, u32[]{:S(2)}, u32[]{:S(2)}) %collective-permute-start.1) | collective-permute-done | bytes 73760 | tf_op jit(solution)/shard_map/ppermute | solution.py:285
  32.1 1.6 %outer.1 = f32[256,128]{1,0:T(8,128)S(1)} custom-call(f32[32,16,128]{2,1,0:T(8,128)S(1)} %get-tuple-element.16.held_ref, f32[9,16,128]{2,1,0:T(8,128)S(1)} %collective-permute-done.lat0_ref, f32[9,16,128]{2,1,0:T(8,128)S(1)} %collective-permute-done.1.lat1_ref, f32[5,32,2,16,128]{4,3,2,1,0:T(8,128)S(1)} %get-tuple-element.24.level1_ref, ...), custom_call_target="tpu_custom_call" | custom-call | flops 4096000 | bytes 1024000 | tf_op jit(solution)/shard_map/outer/pallas_call | solution.py:243
  33.7 18.2 %all_to_all.16 = f32[16,16,128]{2,1,0:T(8,128)S(1)} all-to-all(f32[16,16,128]{2,1,0:T(8,128)S(1)} %bitcast.4), channel_id=1, replica_groups=mesh['mem'=16,'lat'=8,'lon'=4] {'mem'}, dimensions={0} | all-to-all | bytes 262144 | tf_op jit(solution)/shard_map/all_to_all | solution.py:297
  52.0 11.6 %all_to_all.17 = f32[16,16,128]{2,1,0:T(8,128)S(1)} all-to-all(f32[16,16,128]{2,1,0:T(8,128)S(1)} %broadcast_in_dim.2), channel_id=1, replica_groups=mesh['mem'=16,'lat'=8,'lon'=4] {'mem'}, dimensions={0} | all-to-all | bytes 262144 | tf_op jit(solution)/shard_map/all_to_all | solution.py:299
  63.5 0.7 %copy.4 = f32[8,32,128]{2,1,0:T(8,128)} copy(f32[8,32,128]{2,1,0:T(8,128)S(1)} %bitcast.5) | data formatting | bytes 262144
  (3 shorter events, 0.0 us)
Async XLA Ops:
  13.2 11.9 %collective-permute-start = (f32[9,16,128]{2,1,0:T(8,128)S(1)}, f32[9,16,128]{2,1,0:T(8,128)S(1)}, u32[]{:S(2)}, u32[]{:S(2)}) collective-permute-start(f32[9,16,128]{2,1,0:T(8,128)S(1)} %get-tuple-element.19), channel_id=1, source_target_pairs={{0,4},{4,0},{8,12},{12,8},{16,20},{20,16},{24,28},{28,24},{1,5},{5... | collective-permute-start | bytes 221192 | tf_op jit(solution)/shard_map/ppermute | solution.py:284
  21.1 11.0 %collective-permute-start.1 = (f32[9,16,128]{2,1,0:T(8,128)S(1)}, f32[9,16,128]{2,1,0:T(8,128)S(1)}, u32[]{:S(2)}, u32[]{:S(2)}) collective-permute-start(f32[9,16,128]{2,1,0:T(8,128)S(1)} %get-tuple-element.20), channel_id=1, source_target_pairs={{4,8},{8,4},{12,16},{16,12},{20,24},{24,20},{5,9},{9,5},{13,17},{1... | collective-permute-start | bytes 221192 | tf_op jit(solution)/shard_map/ppermute | solution.py:285

commit v3 on v2

v3 whole, which is shorter than its diff:
```python
import math

import jax
import jax.numpy as jnp
from jax import lax
from jax.experimental import pallas as pl
from jax.experimental.pallas import tpu as pltpu
from jax.sharding import PartitionSpec as P

ITERS = 4
factors = (1, 2, 4)
stiffnesses = (1.0, 2.0, 4.0)
weights = (0.5, 0.3, 0.2)
scales = tuple(w / (1.0 + 4.0 * k) for w, k in zip(weights, stiffnesses))

POLY = []
for stiffness in stiffnesses:
    step = stiffness / (1.0 + 4.0 * stiffness)
    series = [step**j for j in range(ITERS)] + [step ** (ITERS - 1) * stiffness]
    POLY.append([[math.comb(i + k, i) * series[i + k] for k in range(ITERS + 1 - i)] for i in range(ITERS + 1)])

LEV = 8
ROWS = 32
LANES = 128
PLANES = 16
GRANT = 16 * 1024 * 1024
EDGE = 9
CORNER = EDGE - 1


def lane_ids():
    return lax.broadcasted_iota(jnp.int32, (PLANES, LANES), 1)


def in_range(lane, start, width):
    return ((lane - start) & (LANES - 1)) < width


def pack_kernel(
    members_hbm, increment_hbm, held_ref, s1_ref, s2_ref, s4_ref, lon_ref, members_ref, increment_ref, wide_ref, sems
):
    lane = lane_ids()
    here, count = lax.axis_index("lon"), lax.axis_size("lon")
    half = LEV * ROWS
    fetches = [pltpu.make_async_copy(increment_hbm, increment_ref, sems.at[0])]
    for m in range(2):
        part = pl.ds(m * half, half)
        fetches.append(pltpu.make_async_copy(members_hbm.at[part], members_ref.at[part], sems.at[1 + m]))
    for fetch in fetches:
        fetch.start()
    fetches[0].wait()
    for m in range(2):
        fetches[1 + m].wait()
        wide_ref[m * half : (m + 1) * half] = members_ref[m * half : (m + 1) * half].astype(jnp.float32)
        for row in range(ROWS):
            inc = increment_ref[pl.ds(row, LEV, stride=ROWS), :] * scales[0]
            value = wide_ref[pl.ds(m * half + row, LEV, stride=ROWS), :]
            held_ref[row, m * LEV : (m + 1) * LEV, :] = value
            s1_ref[row, m * LEV : (m + 1) * LEV, :] = value * inc
    for row in range(ROWS // 2):
        pair = s1_ref[2 * row] + s1_ref[2 * row + 1]
        pair = pair + jnp.where((lane & 1) == 0, pltpu.roll(pair, LANES - 1, 1), pltpu.roll(pair, 1, 1))
        s2_ref[row] = pair * (0.25 * scales[1] / scales[0])
    for row in range(ROWS // 4):
        pair = s2_ref[2 * row] + s2_ref[2 * row + 1]
        pair = pair + jnp.where((lane & 2) == 0, pltpu.roll(pair, LANES - 2, 1), pltpu.roll(pair, 2, 1))
        s4_ref[row] = pair * (0.25 * scales[2] / scales[1])

    tiles = []
    for ref, factor in ((s1_ref, 1), (s2_ref, 2), (s4_ref, 4)):
        width = ITERS * factor
        first = last = jnp.zeros((PLANES, LANES), jnp.float32)
        for row in range(ROWS // factor):
            turned = pltpu.roll(ref[row], width * row, 1) if row else ref[row]
            first = jnp.where(in_range(lane, width * row, width), turned, first)
            last = jnp.where(in_range(lane, width * row - width, width), turned, last)
        tiles.append((first, last))
    even = (lane & 1) == 0
    blank = jnp.zeros((2, PLANES, LANES), jnp.float32)
    lon_ref[here] = blank
    lon_ref[lax.rem(here + 2, count)] = blank
    for side, to in ((0, lax.rem(here + count - 1, count)), (1, lax.rem(here + 1, count))):
        lon_ref[to, 0] = tiles[0][side]
        lon_ref[to, 1] = jnp.where(even, tiles[1][side], tiles[2][side])


def side_tiles(got_ref, lane):
    here, count = lax.axis_index("lon"), lax.axis_size("lon")
    even = (lane & 1) == 0
    out = []
    for of in (lax.rem(here + 1, count), lax.rem(here + count - 1, count)):
        mixed = got_ref[of, 1]
        out.append(
            (
                got_ref[of, 0],
                jnp.where(even, mixed, pltpu.roll(mixed, 1, 1)),
                jnp.where(even, pltpu.roll(mixed, LANES - 1, 1), mixed),
            )
        )
    return out


def beside(right, left, lane, width, row, shift=0):
    both = jnp.where(in_range(lane, width * row, LANES // 2), right, left)
    turn = (shift - width * row) % LANES
    return pltpu.roll(both, turn, 1) if turn else both


CORNER_PLACES = ((2, 1, 0), (2, 2, 20), (2, 3, 32), (1, 1, 42), (1, 2, 52), (1, 3, 58), (0, 1, 63), (0, 2, 68), (0, 3, 71))
SHIFTS = {(band, distance): shift for band, distance, shift in CORNER_PLACES}


def corner_kernel(got_ref, s1_ref, s2_ref, s4_ref, out0_ref, out1_ref):
    lane = lane_ids()
    even = (lane & 1) == 0
    is_odd = (lane * 0 + lax.rem(lax.axis_index("lat"), 2)) == 1
    right, left = side_tiles(got_ref, lane)

    def put(k, tail, head):
        out0_ref[k] = jnp.where(is_odd, head, tail)
        out1_ref[k] = jnp.where(is_odd, tail, head)

    for k in range(ITERS):
        put(k, s1_ref[ROWS - ITERS + k], s1_ref[k])
        tail = jnp.where(even, s2_ref[ROWS // 2 - ITERS + k], s4_ref[ROWS // 4 - ITERS + k])
        put(ITERS + k, tail, jnp.where(even, s2_ref[k], s4_ref[k]))
    made = []
    for tail in (True, False):
        tile = jnp.zeros((PLANES, LANES), jnp.float32)
        for band, distance, shift in CORNER_PLACES:
            factor = factors[band]
            width = factor * (ITERS - distance)
            row = ROWS // factor - distance if tail else distance - 1
            halo = beside(right[band], left[band], lane, ITERS * factor, row, shift)
            tile = jnp.where(in_range(lane, shift - width, 2 * width), halo, tile)
        made.append(tile)
    put(CORNER, *made)


def beside_sum(row, factor, lane, halves=(0, 1)):
    first, last = lane < factor, lane >= LANES - factor
    out = []
    for h in halves:
        up = pltpu.roll(jnp.where(last, row[1 - h], row[h]), factor, 1)
        down = pltpu.roll(jnp.where(first, row[1 - h], row[h]), LANES - factor, 1)
        out.append(up + down)
    return out


def combine(sums, coefficients):
    return sum(c * v for c, v in zip(coefficients, sums))


def inner_kernel(s1_ref, s2_ref, s4_ref, got_ref, *levels_and_sums):
    lane = lane_ids()
    right, left = side_tiles(got_ref, lane)
    bands = len(factors)
    levels, columns, halos = (levels_and_sums[bands * n : bands * (n + 1)] for n in range(3))
    for band, factor in enumerate(factors):
        level, own, column, halo, rows = levels[band], (s1_ref, s2_ref, s4_ref)[band], columns[band], halos[band], ROWS // factor
        for row in range(rows):
            halo[row] = beside(right[band], left[band], lane, ITERS * factor, row)
        for k in range(1, ITERS + 1):
            for row in range(rows):
                before = own[row] if k == 1 else column[k - 2, row]
                new = beside_sum((before, halo[row]), factor, lane, (0, 1) if k < ITERS else (0,))
                column[k - 1, row] = new[0]
                if k < ITERS:
                    halo[row] = new[1]
        for row in range(rows):
            sums = [own[row]] + [column[k, row] for k in range(ITERS)]
            for i in range(ITERS + 1):
                level[i, row] = combine(sums, POLY[band][i])
        for i in range(ITERS - 1, -1, -1):
            for row in range(ITERS - i, rows - ITERS + i):
                level[i, row] = level[i, row] + (level[i + 1, row - 1] + level[i + 1, row + 1])


def outer_kernel(held_ref, lat1_ref, lat0_ref, level1_ref, level2_ref, level4_ref, out_ref, edge_ref, ends_ref):
    lane = lane_ids()
    even = (lane & 1) == 0
    place, places = lax.axis_index("lat"), lax.axis_size("lat")
    odd = lax.rem(place, 2)
    edge_ref[0] = lat0_ref[...]
    edge_ref[1] = lat1_ref[...]
    for band, factor in enumerate(factors):
        level, rows = (level1_ref, level2_ref, level4_ref)[band], ROWS // factor
        for top in (True, False):
            edge = edge_ref.at[1 - odd] if top else edge_ref.at[odd]
            keep = jnp.where(place > 0 if top else place < places - 1, 1.0, 0.0).astype(jnp.float32)
            row_at = (lambda d: -d) if top else (lambda d: rows - 1 + d)
            outside = {}
            for distance in range(1, ITERS + 1):
                k = ITERS - distance if top else distance - 1
                if band == 0:
                    value = edge[k]
                else:
                    value = edge[ITERS + k]
                    turned = pltpu.roll(value, 1 if band == 1 else LANES - 1, 1)
                    value = jnp.where(even, value, turned) if band == 1 else jnp.where(even, turned, value)
                if distance < ITERS:
                    shift = SHIFTS[band, distance]
                    halo = pltpu.roll(edge[CORNER], LANES - shift, 1) if shift else edge[CORNER]
                    now, sums = (value, halo), [value]
                    for k in range(1, ITERS + 1 - distance):
                        now = beside_sum(now, factor, lane, (0, 1) if k < ITERS - distance else (0,))
                        sums.append(now[0])
                else:
                    sums = [value]
                outside[distance] = {i: combine(sums, POLY[band][i]) for i in range(distance, ITERS + 1)}
            latest = {row_at(d): outside[d][ITERS] for d in outside}
            for i in range(ITERS - 1, -1, -1):
                load = lambda row: latest[row] if row in latest else level[i + 1, row]
                new = {}
                for distance in range(i + 1 - ITERS, i + 1):
                    row = row_at(distance)
                    near = load(row - 1) + load(row + 1)
                    new[row] = (outside[distance][i] + near) * keep if distance > 0 else level[i, row] + near
                latest = new
            for row in range(ITERS):
                ends_ref[band, row if top else ITERS + row] = latest[row if top else rows - ITERS + row]

    def final(band, row):
        rows = ROWS // factors[band]
        if row < ITERS:
            return ends_ref[band, row]
        if row >= rows - ITERS:
            return ends_ref[band, row - rows + 2 * ITERS]
        return (level1_ref, level2_ref, level4_ref)[band][0, row]

    for row in range(ROWS):
        total = (final(0, row) + final(1, row // 2) + final(2, row // 4)) * held_ref[row]
        out_ref[pl.ds(row, LEV, stride=ROWS), :] = total[:LEV] + total[LEV:]


def tiles_of(*dims):
    return pltpu.VMEM(dims + (PLANES, LANES), jnp.float32)


def on_chip(kernel, name, out_shape, scratch_shapes=(), held_in=pltpu.VMEM, bundles=1000):
    several = isinstance(out_shape, tuple)
    spec = pl.BlockSpec(memory_space=pltpu.VMEM)

    def call(*operands):
        return pl.pallas_call(
            kernel,
            out_shape=out_shape,
            in_specs=[spec if held_in == pltpu.VMEM else pl.BlockSpec(memory_space=pl.ANY)] * len(operands),
            out_specs=(spec,) * len(out_shape) if several else spec,
            scratch_shapes=scratch_shapes,
            compiler_params=pltpu.CompilerParams(vmem_limit_bytes=GRANT),
            cost_estimate=pl.CostEstimate(flops=bundles * 4096, bytes_accessed=bundles * 1024, transcendentals=0),
            name=name,
        )(*[pltpu.with_memory_space_constraint(x, held_in) for x in operands])

    return call


def body(members, increment):
    columns = lax.axis_size("lon")
    parts = lax.axis_size("mem")
    rows_of = lax.axis_size("lat")
    held, s1, s2, s4, to_lon = on_chip(
        pack_kernel,
        "pack",
        (
            tiles_of(ROWS),
            tiles_of(ROWS),
            tiles_of(ROWS // 2),
            tiles_of(ROWS // 4),
            tiles_of(columns, 2),
        ),
        [
            pltpu.VMEM((2 * LEV * ROWS, LANES), jnp.bfloat16),
            pltpu.VMEM((LEV * ROWS, LANES), jnp.float32),
            pltpu.VMEM((2 * LEV * ROWS, LANES), jnp.float32),
            pltpu.SemaphoreType.DMA((3,)),
        ],
        held_in=pltpu.HBM,
    )(members.reshape(2 * LEV * ROWS, LANES), increment.reshape(LEV * ROWS, LANES))
    from_lon = lax.all_to_all(to_lon, "lon", 0, 0)
    out0, out1 = on_chip(corner_kernel, "corner", (tiles_of(EDGE), tiles_of(EDGE)))(from_lon, s1, s2, s4)
    swap0 = [(i, i ^ 1) for i in range(rows_of)]
    swap1 = [(i, ((i + 1) ^ 1) - 1) for i in range(1, rows_of - 1)]
    in1 = lax.ppermute(out1, "lat", swap1)
    in0 = lax.ppermute(out0, "lat", swap0)
    levels = on_chip(
        inner_kernel,
        "inner",
        tuple(tiles_of(ITERS + 1, ROWS // factor) for factor in factors),
        [tiles_of(ITERS, ROWS // factor) for factor in factors] + [tiles_of(ROWS // factor) for factor in factors],
        bundles=3000,
    )(s1, s2, s4, from_lon)
    partial_value = on_chip(
        outer_kernel,
        "outer",
        pltpu.VMEM((LEV * ROWS, LANES), jnp.float32),
        [tiles_of(2, EDGE), tiles_of(3, 2 * ITERS)],
    )(held, in1, in0, *levels)
    member_count = members.shape[0] * parts
    chunk = (parts, LEV * ROWS // parts, LANES)
    mine = jnp.sum(lax.all_to_all(partial_value.reshape(chunk), "mem", 0, 0), axis=0)
    mine = mine * (1.0 / (member_count - 1))
    whole = lax.all_to_all(jnp.broadcast_to(mine[None], chunk), "mem", 0, 0)
    return whole.reshape(LEV, ROWS, LANES)


def solution(mesh):
    return jax.shard_map(
        body,
        mesh=mesh,
        in_specs=(P("mem", None, "lat", "lon"), P(None, "lat", "lon")),
        out_specs=P(None, "lat", "lon"),
        check_vma=False,
    )
```

time: 64.5 us -> 63 us (0.977)
  waiting for transfers between devices: 7.08 us -> 5.1 us
  blocking collectives: 41.2 us -> 42.4 us
  Pallas kernels: 5.07 us -> 4.34 us
    ppermute x1, waiting for transfers between devices: 7.07 us -> 0.01 us  [body(): in1 = lax.ppermute(out1, 'lat', swap1)]
    ppermute x1, starting transfers between devices: 7.94 us -> 1.92 us  [body(): in0 = lax.ppermute(out0, 'lat', swap0)]
    ppermute x1, starting transfers between devices: 2.19 us -> 8.2 us  [body(): in1 = lax.ppermute(out1, 'lat', swap1)]
    ppermute x1, waiting for transfers between devices: 0.01 us -> 5.09 us  [body(): in0 = lax.ppermute(out0, 'lat', swap0)]
    all_to_all x1, blocking collectives: 18.2 us -> 19.5 us  [body(): lax.all_to_all(partial_value.reshape(chunk), 'mem', 0, 0)]
    pallas_call x4, Pallas kernels: 5.07 us -> 4.34 us  [call(): pl.pallas_call(kernel, out_shape=out_shape, in_specs=[spec if held_in ==...]
where the time goes in v3:
time: 63 us; the launch traced here: 62.7 us
  blocking collectives  42.4 us (67%)
  starting transfers between devices  10.1 us (16%)
  waiting for transfers between devices  5.1 us (8%)
  Pallas kernels  4.34 us (7%)
  local copies, waits for them, and re-layouts  0.67 us (1%)
    all_to_all x1, blocking collectives, body(): lax.all_to_all(partial_value.reshape(chunk), 'mem', 0, 0)  19.5 us
    all_to_all x1, blocking collectives, body(): whole = lax.all_to_all(jnp.broadcast_to(mine[None], chunk), 'mem', 0, 0)  11.6 us
    all_to_all x1, blocking collectives, body(): from_lon = lax.all_to_all(to_lon, 'lon', 0, 0)  11.4 us
    ppermute x1, starting transfers between devices, body(): in1 = lax.ppermute(out1, 'lat', swap1)  8.2 us
    ppermute x1, waiting for transfers between devices, body(): in0 = lax.ppermute(out0, 'lat', swap0)  5.09 us
    pallas_call x4, Pallas kernels, call(): pl.pallas_call(kernel, out_shape=out_shape, in_specs=[spec if held_in ==...  4.34 us
    ppermute x1, starting transfers between devices, body(): in0 = lax.ppermute(out0, 'lat', swap0)  1.92 us
  transfers between devices with their start and end apart: 2, of which 1 were waited for; matrix products, arithmetic and copies ran while one was open for 0% of the time, Pallas kernels for 3%

profile of v3, /device:TPU:7, one launch (start us, length us, event | category | flops | bytes accessed | tf_op | source)
XLA Modules:
  0.0 62.7 jit_solution(14088015234874894892)
XLA Ops:
  0.0 1.5 %pack.1 = (f32[32,16,128]{2,1,0:T(8,128)S(1)}, f32[32,16,128]{2,1,0:T(8,128)S(1)}, f32[16,16,128]{2,1,0:T(8,128)S(1)}, f32[8,16,128]{2,1,0:T(8,128)S(1)}, f32[4,2,16,128]{3,2,1,0:T(8,128)S(1)}) custom-call(bf16[512,128]{1,0:T(8,128)(2,1)} %bitcast.6, f32[256,128]{1,0:T(8,128)} %bitcast.7), custom_call_target="tpu_custom_call" | custom-call | flops 4096000 | bytes 1024000 | tf_op jit(solution)/shard_map/pack/pallas_call | solution.py:245
  1.6 11.4 %all_to_all.15.got_ref = f32[4,2,16,128]{3,2,1,0:T(8,128)S(1)} all-to-all(f32[4,2,16,128]{3,2,1,0:T(8,128)S(1)} %get-tuple-element.16), channel_id=1, replica_groups=mesh['mem'=16,'lat'=8,'lon'=4] {'lon'}, dimensions={0} | all-to-all | bytes 131072 | tf_op jit(solution)/shard_map/all_to_all | solution.py:281
  12.9 0.2 corner.1
  13.1 8.2 %collective-permute-start = (f32[9,16,128]{2,1,0:T(8,128)S(1)}, f32[9,16,128]{2,1,0:T(8,128)S(1)}, u32[]{:S(2)}, u32[]{:S(2)}) collective-permute-start(f32[9,16,128]{2,1,0:T(8,128)S(1)} %get-tuple-element.20), channel_id=1, source_target_pairs={{4,8},{8,4},{12,16},{16,12},{20,24},{24,20},{5,9},{9,5},{13,17},{1... | collective-permute-start | bytes 221192 | tf_op jit(solution)/shard_map/ppermute | solution.py:285
  21.3 1.9 %collective-permute-start.1 = (f32[9,16,128]{2,1,0:T(8,128)S(1)}, f32[9,16,128]{2,1,0:T(8,128)S(1)}, u32[]{:S(2)}, u32[]{:S(2)}) collective-permute-start(f32[9,16,128]{2,1,0:T(8,128)S(1)} %get-tuple-element.21), channel_id=1, source_target_pairs={{0,4},{4,0},{8,12},{12,8},{16,20},{20,16},{24,28},{28,24},{1,5},{5... | collective-permute-start | bytes 221192 | tf_op jit(solution)/shard_map/ppermute | solution.py:286
  23.2 2.0 %inner.1 = (f32[5,32,16,128]{3,2,1,0:T(8,128)S(1)}, f32[5,16,16,128]{3,2,1,0:T(8,128)S(1)}, f32[5,8,16,128]{3,2,1,0:T(8,128)S(1)}) custom-call(f32[32,16,128]{2,1,0:T(8,128)S(1)} %get-tuple-element.17.s1_ref, f32[16,16,128]{2,1,0:T(8,128)S(1)} %get-tuple-element.18.s2_ref, f32[8,16,128]{2,1,0:T(8,128)S(1)} %get-tuple-element.19.s4_ref, ...), custom_call_target="tpu_custom_call" | custom-call | flops 12288000 | bytes 3072000 | tf_op jit(solution)/shard_map/inner/pallas_call | solution.py:245
  25.2 0.0 collective-permute-done.lat1_ref
  25.2 5.1 %collective-permute-done.1.lat0_ref = f32[9,16,128]{2,1,0:T(8,128)S(1)} collective-permute-done((f32[9,16,128]{2,1,0:T(8,128)S(1)}, f32[9,16,128]{2,1,0:T(8,128)S(1)}, u32[]{:S(2)}, u32[]{:S(2)}) %collective-permute-start.1) | collective-permute-done | bytes 73760 | tf_op jit(solution)/shard_map/ppermute | solution.py:286
  30.3 0.7 %outer.1 = f32[256,128]{1,0:T(8,128)S(1)} custom-call(f32[32,16,128]{2,1,0:T(8,128)S(1)} %get-tuple-element.15.held_ref, f32[9,16,128]{2,1,0:T(8,128)S(1)} %collective-permute-done.lat1_ref, f32[9,16,128]{2,1,0:T(8,128)S(1)} %collective-permute-done.1.lat0_ref, f32[5,32,16,128]{3,2,1,0:T(8,128)S(1)} %get-tuple-element.22.level1_ref, ...), custom_call_target="tpu_custom_call" | custom-call | flops 4096000 | bytes 1024000 | tf_op jit(solution)/shard_map/outer/pallas_call | solution.py:245
  31.0 19.5 %all_to_all.16 = f32[16,16,128]{2,1,0:T(8,128)S(1)} all-to-all(f32[16,16,128]{2,1,0:T(8,128)S(1)} %bitcast.4), channel_id=1, replica_groups=mesh['mem'=16,'lat'=8,'lon'=4] {'mem'}, dimensions={0} | all-to-all | bytes 262144 | tf_op jit(solution)/shard_map/all_to_all | solution.py:302
  50.5 11.6 %all_to_all.17 = f32[16,16,128]{2,1,0:T(8,128)S(1)} all-to-all(f32[16,16,128]{2,1,0:T(8,128)S(1)} %broadcast_in_dim.2), channel_id=1, replica_groups=mesh['mem'=16,'lat'=8,'lon'=4] {'mem'}, dimensions={0} | all-to-all | bytes 262144 | tf_op jit(solution)/shard_map/all_to_all | solution.py:304
  62.1 0.7 %copy.4 = f32[8,32,128]{2,1,0:T(8,128)} copy(f32[8,32,128]{2,1,0:T(8,128)S(1)} %bitcast.5) | data formatting | bytes 262144
  (3 shorter events, 0.0 us)
Async XLA Ops:
  13.1 12.1 %collective-permute-start = (f32[9,16,128]{2,1,0:T(8,128)S(1)}, f32[9,16,128]{2,1,0:T(8,128)S(1)}, u32[]{:S(2)}, u32[]{:S(2)}) collective-permute-start(f32[9,16,128]{2,1,0:T(8,128)S(1)} %get-tuple-element.20), channel_id=1, source_target_pairs={{4,8},{8,4},{12,16},{16,12},{20,24},{24,20},{5,9},{9,5},{13,17},{1... | collective-permute-start | bytes 221192 | tf_op jit(solution)/shard_map/ppermute | solution.py:285
  21.3 9.0 %collective-permute-start.1 = (f32[9,16,128]{2,1,0:T(8,128)S(1)}, f32[9,16,128]{2,1,0:T(8,128)S(1)}, u32[]{:S(2)}, u32[]{:S(2)}) collective-permute-start(f32[9,16,128]{2,1,0:T(8,128)S(1)} %get-tuple-element.21), channel_id=1, source_target_pairs={{0,4},{4,0},{8,12},{12,8},{16,20},{20,16},{24,28},{28,24},{1,5},{5... | collective-permute-start | bytes 221192 | tf_op jit(solution)/shard_map/ppermute | solution.py:286
